TPU v7x, 32 devices: a whole 2x2x4 slice. The times are simulated.
32 devices in a mesh: main: 4 (over y, core), sub: 8 (over z, x).
Axes of the slice: x: 2, y: 2, z: 4, core: 2. Of those that a mesh axis runs over, the one named last changes fastest.
Arguments:
- byte_states: bfloat16 [16384, 1024], P(('main', 'sub')), may hold values from -8 to 8
- boundary_flags: int32 [16384], P(('main', 'sub')), may hold values from 0 to 1, as said below
- span_counts: int32 [32], replicated, may hold values from 2 to 96, as said below
- enc_norm_gain: float32 [1024], replicated, may hold values from 0.5 to 1.5
- mamba_in: bfloat16 [1024, 4096], replicated, may hold values from -0.1875 to 0.1875
- mamba_bc: bfloat16 [1024, 256], replicated, may hold values from -0.03125 to 0.03125
- mamba_dt: bfloat16 [1024, 32], replicated, may hold values from -0.1875 to 0.1875
- dt_bias: float32 [32], replicated, may hold values from -3 to 0.5
- decay_rate: float32 [32], replicated, may hold values from 0.00024414062 to 0.1
- skip_gain: float32 [32], replicated, may hold values from 1 to 10
- gate_norm_gain: float32 [2048], replicated, may hold values from 0.5 to 1.5
- mamba_out: bfloat16 [2048, 1024], replicated, may hold values from -0.125 to 0.125
- down_proj: bfloat16 [1024, 2048], replicated, may hold values from -0.1875 to 0.1875
- attn_norm_gain: float32 [2048], replicated, may hold values from 0.5 to 1.5
- qkv_weight: bfloat16 [2048, 16, 384], P(None, 'sub'), may hold values from -8 to 8
- out_weight: bfloat16 [16, 128, 2048], P('sub'), may hold values from -0.125 to 0.125
- up_proj: bfloat16 [2048, 1024], replicated, may hold values from -0.125 to 0.125
Outputs:
- byte_out: bfloat16 [16384, 1024], P(('main', 'sub'))
Inputs may be any that keep to these rules, and one draw needn't show every extreme that they name: `boundary_flags`: each device's block of 512 bytes holds between 2 and 96 flagged bytes, and some block holds exactly 96; the first byte of the sequence is flagged. span_counts[d] is the number of flagged bytes in block d.
All inputs are finite; a program needn't handle non-finite values.
Results may differ from a plain program's by a relative error of at most 0.012.
Values may be sent and summed in bfloat16 or wider, within the bound.
No kernel may reach another device: no remote copies, remote signals or barrier semaphores. Data moves between devices by JAX's collectives and lax.ppermute only.
A program may use at most 384 MiB of HBM per device.

v0:
```python
import functools
import math

import jax
import jax.numpy as jnp
from jax import lax
from jax.experimental import pallas as pl
from jax.experimental.pallas import tpu as pltpu
from jax.sharding import PartitionSpec as P


INNER_WIDTH = 2048
HEAD_COUNT = 32
HEAD_WIDTH = 64
STATE = 128
HD = 128
CAP = 96
CHUNK = 128
LANES = 128
QUAD = 256
STATE_STEP = 1024
FINISH_STEP = 1024
EXTRA = 16

epsilon = 1e-06
highest = lax.Precision.HIGHEST
LOG2E = math.log2(math.e)
BF = jnp.bfloat16
F32 = jnp.float32


def dot(a, b, **kw):
    return jnp.dot(a, b, preferred_element_type=F32, **kw)


def dot_t(a, b):
    return lax.dot_general(a, b, (((1,), (1,)), ((), ())), preferred_element_type=F32)


def silu(v):
    return v * jax.nn.sigmoid(v)


def params(**kw):
    return pltpu.CompilerParams(dimension_semantics=("arbitrary",), **kw)


def cost(us):
    return pl.CostEstimate(flops=int(us * 6e8), transcendentals=0, bytes_accessed=int(us * 3e6))


def whole(shape):
    rank = len(shape)
    return pl.BlockSpec(shape, lambda j: (0,) * rank)


def pair_lanes(columns, pair):
    rows = columns.shape[0]
    low = jnp.broadcast_to(columns[:, 2 * pair : 2 * pair + 1], (rows, LANES))
    high = jnp.broadcast_to(columns[:, 2 * pair + 1 : 2 * pair + 2], (rows, LANES))
    lane = lax.broadcasted_iota(jnp.int32, (rows, LANES), 1)
    return jnp.where(lane < HEAD_WIDTH, low, high)


def padded(row_ref):
    return jnp.concatenate([row_ref[...], jnp.zeros((1, LANES - HEAD_COUNT), F32)], 1)


def step_columns(table, j, width):
    return pltpu.roll(table, (LANES - width // HEAD_WIDTH * j) % LANES, 1)


def states_body(
    bytes_ref, gain_ref, wx_ref, wbc_ref, wdt_ref, bias_ref, rate_ref,
    normed_ref, x_ref, bc_ref, cum_ref, chunk_ref, late_ref, send_ref,
    bt_ref, weight_ref, total_ref,
):
    j = pl.program_id(0)
    rows = bytes_ref.shape[0]
    chunks = rows // CHUNK

    @pl.when(j == 0)
    def _():
        values = bytes_ref[...].astype(F32)
        scale = lax.rsqrt(jnp.mean(values * values, -1, keepdims=True) + epsilon)
        normed = (values * scale * gain_ref[...]).astype(BF)
        normed_ref[...] = normed
        bc = dot(normed, wbc_ref[...])
        bc_ref[...] = bc.astype(BF)
        spare = jnp.zeros((LANES - HEAD_COUNT, normed.shape[1]), BF)
        raw = dot_t(normed, jnp.concatenate([wdt_ref[...], spare], 0)) + padded(bias_ref)
        dt = jnp.maximum(raw, 0.0) + jnp.log1p(jnp.exp(-jnp.abs(raw)))
        step = dt * (-LOG2E * padded(rate_ref))
        row = lax.broadcasted_iota(jnp.int32, (CHUNK, CHUNK), 0)
        col = lax.broadcasted_iota(jnp.int32, (CHUNK, CHUNK), 1)
        lower = (row >= col).astype(F32)
        log_dt = jnp.log(dt) * LOG2E
        end = jnp.zeros((1, LANES), F32)
        lates = []
        for c in range(chunks):
            at = pl.ds(c * CHUNK, CHUNK)
            part = slice(c * CHUNK, (c + 1) * CHUNK)
            within = jnp.dot(lower, step[part], precision=highest, preferred_element_type=F32)
            cum = within + end
            cum_ref[at, :] = cum
            late = cum - log_dt[part]
            lates.append(late)
            turned = late.T
            for quad in range(HEAD_COUNT // 4):
                late_ref[quad, 0:4, at] = turned[4 * quad : 4 * quad + 4]
            end = cum[CHUNK - 1 :, :]
            chunk_ref[at, :] = jnp.exp2(end - late)
            bt_ref[:, at] = bc[part, :STATE].T.astype(BF)
        for c in range(chunks):
            weight_ref[pl.ds(c * CHUNK, CHUNK), :] = jnp.exp2(end - lates[c])
        total_ref[...] = jnp.broadcast_to(jnp.exp2(end), total_ref.shape)

    x = silu(dot(normed_ref[...], wx_ref[...]))
    x_ref[...] = x.astype(BF)
    weight = step_columns(weight_ref[...], j, STATE_STEP)
    factor = step_columns(total_ref[...], j, STATE_STEP)
    spread = jnp.concatenate([pair_lanes(weight, pair) for pair in range(STATE_STEP // LANES)], 1)
    state = dot(bt_ref[...], (x * spread).astype(BF))
    group = send_ref.shape[0] * LANES // STATE_STEP
    piece = send_ref.shape[1] - EXTRA
    for pair in range(STATE_STEP // LANES):
        lanes = slice(pair * LANES, (pair + 1) * LANES)
        decay = pair_lanes(factor, pair)[:1]
        high = decay.astype(BF).astype(F32)
        row = lax.broadcasted_iota(jnp.int32, (EXTRA, LANES), 0)
        tail = jnp.where(row == 0, high, jnp.where(row == 1, decay - high, 0.0)).astype(BF)
        for d in range(group):
            part = slice(d * piece, (d + 1) * piece)
            send_ref[pair * group + d, :piece, :] = state[part, lanes].astype(BF)
            send_ref[pair * group + d, piece:, :] = tail


def scan_states(byte_states, gain, mamba_in, mamba_bc, mamba_dt, bias, rate, devices):
    rows, width = byte_states.shape
    steps = INNER_WIDTH // STATE_STEP
    piece = INNER_WIDTH * STATE // (LANES * devices)
    return pl.pallas_call(
        states_body,
        grid=(steps,),
        in_specs=[
            whole((rows, width)),
            whole((1, width)),
            pl.BlockSpec((width, STATE_STEP), lambda j: (0, j)),
            whole((width, 2 * STATE)),
            whole((HEAD_COUNT, width)),
            whole((1, HEAD_COUNT)),
            whole((1, HEAD_COUNT)),
        ],
        out_specs=[
            whole((rows, width)),
            pl.BlockSpec((rows, STATE_STEP), lambda j: (0, j)),
            whole((rows, 2 * STATE)),
            whole((rows, LANES)),
            whole((rows, LANES)),
            whole((HEAD_COUNT // 4, 8, rows)),
            pl.BlockSpec((devices // steps, piece + EXTRA, LANES), lambda j: (j, 0, 0)),
        ],
        out_shape=[
            jax.ShapeDtypeStruct((rows, width), BF),
            jax.ShapeDtypeStruct((rows, INNER_WIDTH), BF),
            jax.ShapeDtypeStruct((rows, 2 * STATE), BF),
            jax.ShapeDtypeStruct((rows, LANES), F32),
            jax.ShapeDtypeStruct((rows, LANES), F32),
            jax.ShapeDtypeStruct((HEAD_COUNT // 4, 8, rows), F32),
            jax.ShapeDtypeStruct((devices, piece + EXTRA, LANES), BF),
        ],
        scratch_shapes=[
            pltpu.VMEM((STATE, rows), BF),
            pltpu.VMEM((rows, LANES), F32),
            pltpu.VMEM((8, LANES), F32),
        ],
        compiler_params=params(),
        cost_estimate=cost(9),
        name="scan_states",
    )(byte_states, gain, mamba_in, mamba_bc, mamba_dt, bias, rate)


def prefix_body(parts_ref, out_ref):
    devices, piece, _ = out_ref.shape
    state = jnp.zeros((piece, LANES), F32)
    for d in range(devices):
        out_ref[d] = state.astype(BF)
        tail = parts_ref[d, piece:, :].astype(F32)
        decay = tail[0:1] + tail[1:2]
        state = state * decay + parts_ref[d, :piece, :].astype(F32)


def state_prefix(parts):
    devices, rows, _ = parts.shape
    piece = rows - EXTRA
    return pl.pallas_call(
        prefix_body,
        grid=(1,),
        in_specs=[whole(parts.shape)],
        out_specs=whole((devices, piece, LANES)),
        out_shape=jax.ShapeDtypeStruct((devices, piece, LANES), BF),
        compiler_params=params(),
        cost_estimate=cost(2),
        name="state_prefix",
    )(parts)


def within_body(
    normed_ref, wg_ref, x_ref, bc_ref, cum_ref, chunk_ref, late_ref, skip_ref,
    yg_ref, grown_ref, contact_ref, bt_ref,
):
    j = pl.program_id(0)
    rows = normed_ref.shape[0]
    chunks = rows // CHUNK

    @pl.when(j == 0)
    def _():
        row = lax.broadcasted_iota(jnp.int32, (CHUNK, CHUNK), 0)
        col = lax.broadcasted_iota(jnp.int32, (CHUNK, CHUNK), 1)
        for c in range(chunks):
            at = pl.ds(c * CHUNK, CHUNK)
            contact = dot_t(bc_ref[at, STATE:], bc_ref[at, :STATE])
            contact_ref[c] = jnp.where(row >= col, contact, 0.0)
            bt_ref[c] = bc_ref[at, :STATE].astype(F32).T.astype(BF)

    gate = silu(dot(normed_ref[...], wg_ref[...]))
    cum = step_columns(cum_ref[...], j, QUAD)
    chunk = step_columns(chunk_ref[...], j, QUAD)
    skip = step_columns(jnp.broadcast_to(padded(skip_ref), (8, LANES)), j, QUAD)
    lane = lax.broadcasted_iota(jnp.int32, (CHUNK, LANES), 1)
    for pair in range(2):
        lanes = slice(pair * LANES, (pair + 1) * LANES)
        skips = pair_lanes(skip, pair)[:1]
        end = jnp.zeros((1, LANES), F32)
        state = None
        for c in range(chunks):
            at = pl.ds(c * CHUNK, CHUNK)
            part = slice(c * CHUNK, (c + 1) * CHUNK)
            weights = []
            for head in (2 * pair, 2 * pair + 1):
                gap = cum[part, head : head + 1] - late_ref[0, head : head + 1, at]
                weights.append((jnp.exp2(jnp.minimum(gap, 126.0)) * contact_ref[c]).astype(BF))
            packed = x_ref[at, lanes]
            zero = jnp.zeros_like(packed)
            stacked = jnp.concatenate(
                [jnp.where(lane < HEAD_WIDTH, packed, zero),
                 jnp.where(lane < HEAD_WIDTH, zero, packed)], 0
            )
            x = packed.astype(F32)
            y = dot(jnp.concatenate(weights, 1), stacked) + skips * x
            spread = pair_lanes(cum[part], pair)
            if c:
                y = y + dot(bc_ref[at, STATE:], state.astype(BF)) * jnp.exp2(spread - end)
            g = gate[part, lanes]
            yg_ref[at, lanes] = (y * g).astype(BF)
            grown_ref[at, lanes] = (jnp.exp2(spread) * g).astype(BF)
            if c + 1 < chunks:
                scaled = (x * pair_lanes(chunk[part], pair)).astype(BF)
                update = dot(bt_ref[c], scaled)
                last = spread[CHUNK - 1 :]
                state = update if c == 0 else state * jnp.exp2(last - end) + update
                end = last


def scan_within(normed, mamba_in, x, bc, cum, chunk, late, skip):
    rows, width = normed.shape
    chunks = rows // CHUNK
    steps = INNER_WIDTH // QUAD
    return pl.pallas_call(
        within_body,
        grid=(steps,),
        in_specs=[
            whole((rows, width)),
            pl.BlockSpec((width, QUAD), lambda j: (0, j + steps)),
            pl.BlockSpec((rows, QUAD), lambda j: (0, j)),
            whole((rows, 2 * STATE)),
            whole((rows, LANES)),
            whole((rows, LANES)),
            pl.BlockSpec((1, 8, rows), lambda j: (j, 0, 0)),
            whole((1, HEAD_COUNT)),
        ],
        out_specs=[pl.BlockSpec((rows, QUAD), lambda j: (0, j))] * 2,
        out_shape=[jax.ShapeDtypeStruct((rows, INNER_WIDTH), BF)] * 2,
        scratch_shapes=[
            pltpu.VMEM((chunks, CHUNK, CHUNK), F32),
            pltpu.VMEM((chunks, STATE, CHUNK), BF),
        ],
        compiler_params=params(),
        cost_estimate=cost(14),
        name="scan_within",
    )(normed, mamba_in, x, bc, cum, chunk, late, skip)


def finish_body(
    yg_ref, grown_ref, c_ref, incoming_ref, gain_ref, wo_ref, bytes_ref, rank_ref, down_ref,
    encoded_ref, main_ref, sent_ref, acc_ref, square_ref, weight_ref, sem,
):
    j = pl.program_id(0)
    rows = yg_ref.shape[0]

    @pl.when(j == 0)
    def _():
        pltpu.make_async_copy(down_ref, weight_ref, sem).start()
        square_ref[...] = jnp.zeros_like(square_ref)

    state = jnp.concatenate([incoming_ref[p] for p in range(incoming_ref.shape[0])], 1)
    carried = dot(c_ref[...], state)
    gated = yg_ref[...].astype(F32) + carried * grown_ref[...].astype(F32)
    parts = [gated[:, p : p + LANES] for p in range(0, FINISH_STEP, LANES)]
    square_ref[...] += sum(part * part for part in parts)
    mixed = dot((gated * gain_ref[...]).astype(BF), wo_ref[...])

    @pl.when(j == 0)
    def _():
        acc_ref[...] = mixed

    @pl.when(j > 0)
    def _():
        acc_ref[...] += mixed

    @pl.when(j == pl.num_programs(0) - 1)
    def _():
        mean = jnp.sum(square_ref[...], -1, keepdims=True) * (1.0 / INNER_WIDTH)
        encoded = (bytes_ref[...].astype(F32) + acc_ref[...] * lax.rsqrt(mean + epsilon)).astype(BF)
        encoded_ref[...] = encoded
        slot = lax.broadcasted_iota(jnp.int32, (CAP, rows), 0)
        picker = jnp.where(rank_ref[...] == slot, 1.0, 0.0).astype(BF)
        spans = dot(picker, encoded)
        pltpu.make_async_copy(down_ref, weight_ref, sem).wait()
        main_in = dot(spans.astype(BF), weight_ref[...]).astype(BF)
        main_ref[...] = main_in
        wide = main_in.astype(F32)
        scale = lax.rsqrt(jnp.mean(wide * wide, -1, keepdims=True) + epsilon)
        sent_ref[...] = (spans * scale).astype(BF)


def scan_finish(yg, grown, bc, incoming, gain, mamba_out, byte_states, rank, down):
    rows, width = byte_states.shape
    steps = INNER_WIDTH // FINISH_STEP
    return pl.pallas_call(
        finish_body,
        grid=(steps,),
        in_specs=[
            pl.BlockSpec((rows, FINISH_STEP), lambda j: (0, j)),
            pl.BlockSpec((rows, FINISH_STEP), lambda j: (0, j)),
            pl.BlockSpec((rows, STATE), lambda j: (0, 1)),
            pl.BlockSpec((FINISH_STEP // LANES, STATE, LANES), lambda j: (j, 0, 0)),
            pl.BlockSpec((1, FINISH_STEP), lambda j: (0, j)),
            pl.BlockSpec((FINISH_STEP, width), lambda j: (j, 0)),
            whole((rows, width)),
            whole((1, rows)),
            pl.BlockSpec(memory_space=pl.ANY),
        ],
        out_specs=[whole((rows, width)), whole((CAP, down.shape[1])), whole((CAP, width))],
        out_shape=[
            jax.ShapeDtypeStruct((rows, width), BF),
            jax.ShapeDtypeStruct((CAP, down.shape[1]), BF),
            jax.ShapeDtypeStruct((CAP, width), BF),
        ],
        scratch_shapes=[
            pltpu.VMEM((rows, width), F32),
            pltpu.VMEM((rows, LANES), F32),
            pltpu.VMEM(down.shape, BF),
            pltpu.SemaphoreType.DMA(()),
        ],
        compiler_params=params(),
        cost_estimate=cost(10),
        name="scan_finish",
    )(yg, grown, bc, incoming, gain, mamba_out, byte_states, rank, down)


def sub_grid(count):
    minor = 1
    while minor * minor * 4 <= count:
        minor *= 2
    return count // minor, minor


def sub_move(value, axis, dz, dx):
    count = lax.axis_size(axis)
    major, minor = sub_grid(count)
    route = []
    for i in range(count):
        z, x = divmod(i, minor)
        route.append((i, (z + dz) % major * minor + (x + dx) % minor))
    return lax.ppermute(value, axis, route)


def gather_columns(block, axis):
    major, _ = sub_grid(lax.axis_size(axis))
    return [block] + [sub_move(block, axis, dz, 0) for dz in range(1, major)]


def gather_rest(columns, axis):
    _, minor = sub_grid(lax.axis_size(axis))
    return columns + [sub_move(c, axis, 0, dx) for dx in range(1, minor) for c in columns]


def sub_sources(axis):
    count = lax.axis_size(axis)
    major, minor = sub_grid(count)
    me = lax.axis_index(axis)
    z, x = me // minor, me % minor
    return [(z - dz) % major * minor + (x - dx) % minor
            for dx in range(minor) for dz in range(major)]


def partner(value, axis):
    count = lax.axis_size(axis)
    return lax.ppermute(value, axis, [(i, i ^ 1) for i in range(count)])


def gather_main(block, axis):
    count = lax.axis_size(axis)
    near = [block] + [
        lax.ppermute(block, axis, [(i, (i + k) % count) for i in range(count)])
        for k in range(2, count, 2)
    ]
    near = jnp.stack(near)
    return near, partner(near, axis)


def main_sources(axis):
    count = lax.axis_size(axis)
    me = lax.axis_index(axis)
    return [(m - k) % count for m in (me, me ^ 1) for k in range(0, count, 2)]


def qkv_body(weight_ref, *refs):
    *pieces, q_ref, kv_ref = refs
    rows = jnp.concatenate([piece[...] for piece in pieces], 0)
    for h in range(weight_ref.shape[1] // (3 * HD)):
        out = dot(rows, weight_ref[:, h * 3 * HD : (h + 1) * 3 * HD])
        q_ref[:, h * HD : (h + 1) * HD] = (out[:, :HD] * (HD**-0.5 * LOG2E)).astype(BF)
        kv_ref[:, h * 2 * HD : (h + 1) * 2 * HD] = out[:, HD:].astype(BF)


def vmem(count):
    return [pl.BlockSpec(memory_space=pltpu.VMEM)] * count


SCALARS = pl.BlockSpec(memory_space=pltpu.SMEM)


def project_qkv(weight, pieces):
    slots = pieces[0].shape[0] * len(pieces)
    heads = weight.shape[1] // (3 * HD)
    return pl.pallas_call(
        qkv_body,
        in_specs=vmem(1 + len(pieces)),
        out_specs=vmem(2),
        out_shape=[
            jax.ShapeDtypeStruct((slots, heads * HD), BF),
            jax.ShapeDtypeStruct((slots, heads * 2 * HD), BF),
        ],
        cost_estimate=cost(4),
        name="project_qkv",
    )(weight, *pieces)


def place(out_ref, index_ref, parts):
    first = index_ref.shape[0] - out_ref.shape[0] // CAP
    for part in parts:
        for p in range(part.shape[0] // CAP):
            at = pl.multiple_of(index_ref[first] * CAP, 32)
            out_ref[pl.ds(at, CAP), :] = part[p * CAP : (p + 1) * CAP, :]
            first += 1


def span_up_body(
    index_ref, edge_ref, main_up_ref, heads_ref, own_ref, other_ref, up_ref, edges_ref, columns_ref
):
    subs, cap, _ = heads_ref.shape
    half = own_ref.shape[0]
    mains = 2 * half
    flat = jnp.concatenate([heads_ref[index_ref[1 + mains + r]] for r in range(subs)], 1)
    for p in range(half):
        columns_ref[index_ref[1 + p]] = dot(flat, own_ref[p])
        columns_ref[index_ref[1 + half + p]] = dot(flat, other_ref[p])
    joined = jnp.concatenate([columns_ref[p] for p in range(mains)], 1)
    up = (main_up_ref[...] + joined).astype(BF)
    up_ref[...] = up
    slot = lax.broadcasted_iota(jnp.int32, (16, cap), 1)
    row = lax.broadcasted_iota(jnp.int32, (16, cap), 0)
    picker = jnp.where((slot == edge_ref[0] - 2 + row) & (row < 2), 1.0, 0.0).astype(BF)
    edges_ref[...] = dot(picker, up).astype(BF)


def project_up(index, main_up, heads, weights, own_count):
    cap, width = main_up.shape
    half, _, part = weights[0].shape
    return pl.pallas_call(
        span_up_body,
        in_specs=[SCALARS, SCALARS] + vmem(4),
        out_specs=vmem(2),
        out_shape=[
            jax.ShapeDtypeStruct((cap, width), BF),
            jax.ShapeDtypeStruct((16, width), BF),
        ],
        scratch_shapes=[pltpu.VMEM((2 * half, cap, part), F32)],
        cost_estimate=cost(5),
        name="project_up",
    )(index, own_count, main_up, heads, *weights)


BLOCK = 256


def scores_of(q, kv_ref, bias, head, span):
    return dot_t(q, kv_ref[:span, head * 2 * HD : head * 2 * HD + HD]) + bias[:, :span]


def mixed_of(numer, kv_ref, head, span):
    return dot(numer.astype(BF), kv_ref[:span, head * 2 * HD + HD : (head + 1) * 2 * HD])


def join(carry, q, kv_refs, biases, head):
    top, total, acc = carry
    slots = kv_refs[0].shape[0]
    scores = [scores_of(q, kv, bias, head, slots) for kv, bias in zip(kv_refs, biases)]
    new = top
    for s in scores:
        new = jnp.maximum(new, jnp.max(s, -1, keepdims=True))
    rescale = jnp.exp2(top - new)
    total, acc = total * rescale, acc * rescale
    for s, kv in zip(scores, kv_refs):
        numer = jnp.exp2(s - new)
        total = total + jnp.sum(numer, -1, keepdims=True)
        acc = acc + mixed_of(numer, kv, head, slots)
    return new, total, acc


def store(stats_ref, acc_ref, at, head, carry):
    top, total, acc = carry
    acc_ref[at, head * HD : (head + 1) * HD] = acc
    stats_ref[2 * head, at, :] = jnp.broadcast_to(top, acc.shape)
    stats_ref[2 * head + 1, at, :] = jnp.broadcast_to(total, acc.shape)


def near_body(index_ref, bias_ref, *refs):
    *parts, q_ref, stats_ref, acc_ref, kv_ref, other_ref = refs
    count = len(parts) // 3
    place(q_ref, index_ref, parts[:count])
    place(kv_ref, index_ref, parts[count : 2 * count])
    pl.when(index_ref[0] % 2 == 1)(lambda: place(other_ref, index_ref, parts[2 * count :]))
    slots = q_ref.shape[0]
    heads = q_ref.shape[1] // HD
    mine = index_ref[0]

    def own(at, b, head):
        span = (b + 1) * BLOCK
        q = q_ref[at, head * HD : (head + 1) * HD]
        scores = scores_of(q, kv_ref, bias_ref[mine], head, span)
        row = lax.broadcasted_iota(jnp.int32, scores.shape, 0) + b * BLOCK
        col = lax.broadcasted_iota(jnp.int32, scores.shape, 1)
        scores = jnp.where(col <= row, scores, -2e30)
        top = jnp.max(scores, -1, keepdims=True)
        numer = jnp.exp2(scores - top)
        return top, jnp.sum(numer, -1, keepdims=True), mixed_of(numer, kv_ref, head, span)

    def run(paired):
        for b in range(slots // BLOCK):
            at = pl.ds(b * BLOCK, BLOCK)
            for head in range(heads):
                carry = own(at, b, head)
                if paired:
                    q = q_ref[at, head * HD : (head + 1) * HD]
                    carry = join(carry, q, [other_ref], [bias_ref[mine - 1]], head)
                store(stats_ref, acc_ref, at, head, carry)

    pl.when(mine % 2 == 1)(lambda: run(True))
    pl.when(mine % 2 == 0)(lambda: run(False))


def near_attention(index, bias, queries, keys, others):
    slots = bias.shape[2]
    width = queries[0].shape[1]
    parts = [*queries, *keys, *others]
    return pl.pallas_call(
        near_body,
        in_specs=[SCALARS] + vmem(1 + len(parts)),
        out_specs=vmem(3),
        out_shape=[
            jax.ShapeDtypeStruct((slots, width), BF),
            jax.ShapeDtypeStruct((2 * width // HD, slots, HD), F32),
            jax.ShapeDtypeStruct((slots, width), F32),
        ],
        scratch_shapes=[pltpu.VMEM((slots, 2 * width), BF)] * 2,
        cost_estimate=cost(9),
        name="near_attention",
    )(index, bias, *parts)


def far_body(index_ref, q_ref, stats_in, acc_in, bias_ref, *refs, shards):
    parts, (out_ref, stats_ref, acc_ref, *pieces) = refs[: -3 - shards], refs[-3 - shards :]
    slots = q_ref.shape[0]
    heads = q_ref.shape[1] // HD
    mine = index_ref[0]
    steps = shards // 2
    count = len(parts) // shards

    @pl.when(mine >= 2)
    def _():
        for p, piece in enumerate(pieces):
            place(piece, index_ref, parts[p * count : (p + 1) * count])

    def finish(at, head, carry):
        out_ref[at, head * HD : (head + 1) * HD] = (carry[2] / carry[1]).astype(BF)

    def each(refs, act):
        for b in range(slots // BLOCK):
            at = pl.ds(b * BLOCK, BLOCK)
            for head in range(heads):
                acc = refs[1][at, head * HD : (head + 1) * HD]
                act(at, head, (refs[0][2 * head, at, :1], refs[0][2 * head + 1, at, :1], acc))

    for k in range(steps):
        def act(at, head, carry, k=k):
            sources = (mine - 2 * (k + 1), mine + 1 - 2 * (mine % 2) - 2 * (k + 1))
            q = q_ref[at, head * HD : (head + 1) * HD]
            biases = [bias_ref[source] for source in sources]
            carry = join(carry, q, pieces[2 * k : 2 * k + 2], biases, head)
            last = mine < 2 * (k + 2)
            if k + 1 == steps:
                finish(at, head, carry)
            else:
                pl.when(last)(lambda: finish(at, head, carry))
                pl.when(jnp.logical_not(last))(lambda: store(stats_ref, acc_ref, at, head, carry))

        source_refs = (stats_in, acc_in) if k == 0 else (stats_ref, acc_ref)
        pl.when(mine >= 2 * (k + 1))(functools.partial(each, source_refs, act))

    pl.when(mine < 2)(functools.partial(each, (stats_in, acc_in), finish))


def far_attention(index, q, stats, acc, bias, shards):
    slots, width = q.shape
    parts = [part for shard in shards for part in shard]
    return pl.pallas_call(
        functools.partial(far_body, shards=len(shards)),
        in_specs=[SCALARS] + vmem(4 + len(parts)),
        out_specs=vmem(1)[0],
        out_shape=jax.ShapeDtypeStruct((slots, width), BF),
        scratch_shapes=[pltpu.VMEM(stats.shape, F32), pltpu.VMEM((slots, width), F32)]
        + [pltpu.VMEM((slots, 2 * width), BF)] * len(shards),
        cost_estimate=cost(9),
        name="far_attention",
    )(index, q, stats, acc, bias, *parts)


def far_shards(kv, axis):
    count = lax.axis_size(axis)
    shifts = range(2, count, 2)
    return [lax.ppermute(kv, axis, [(i - k, i) for i in range(k, count)]) for k in shifts]


def local(
    byte_states,
    boundary_flags,
    span_counts,
    enc_norm_gain,
    mamba_in,
    mamba_bc,
    mamba_dt,
    dt_bias,
    decay_rate,
    skip_gain,
    gate_norm_gain,
    mamba_out,
    down_proj,
    attn_norm_gain,
    qkv_weight,
    out_weight,
    up_proj,
):
    axes = ("main", "sub")
    devices = lax.axis_size(axes)
    subs = lax.axis_size("sub")
    mains = lax.axis_size("main")
    main_id = lax.axis_index("main")
    _, width = byte_states.shape
    heads = qkv_weight.shape[1]
    model = qkv_weight.shape[0]

    up_part = width // mains
    up_columns = lax.dynamic_slice_in_dim(up_proj, main_id * up_part, up_part, 1)
    out_up = dot(out_weight.reshape(heads * HD, model), up_columns).astype(BF)
    out_up, byte_states = lax.optimization_barrier((out_up, byte_states))
    out_up = gather_columns(out_up, "sub")

    normed, x, bc, cum, chunk, late, send = scan_states(
        byte_states,
        enc_norm_gain[None],
        mamba_in,
        mamba_bc,
        mamba_dt.T,
        dt_bias[None],
        decay_rate[None],
        devices,
    )
    send, flags, counts, *out_up = lax.optimization_barrier(
        (send, boundary_flags, span_counts, *out_up)
    )
    out_up = gather_rest([jnp.concatenate(out_up, 0)], "sub")
    parts = lax.all_to_all(send, axes, 0, 0, tiled=True)
    yg, grown = scan_within(normed, mamba_in, x, bc, cum, chunk, late, skip_gain[None])
    sub_index = sub_sources("sub")
    index = jnp.stack([main_id] + main_sources("main") + sub_index).astype(jnp.int32)
    slot = jnp.arange(subs * CAP, dtype=jnp.int32)
    valid = slot[None] % CAP < jnp.repeat(counts.reshape(mains, subs), CAP, axis=1)
    bias = jnp.where(valid, 0.0, -1e30).astype(F32)[:, None, :]
    span_rank = jnp.cumsum(flags) - 1
    picked = jnp.where(flags == 1, span_rank, -1)
    device_ids = jnp.arange(devices, dtype=jnp.int32)
    device_id = main_id * subs + lax.axis_index("sub")
    own_count = jnp.sum(jnp.where(device_ids == device_id, counts, 0))[None]
    parts, yg, grown, index, bias, picked, own_count, down, weight, *out_up = (
        lax.optimization_barrier(
            (parts, yg, grown, index, bias, picked, own_count, down_proj, qkv_weight, *out_up)
        )
    )
    out_up = gather_main(jnp.concatenate(out_up, 0), "main")
    incoming = lax.all_to_all(state_prefix(parts), axes, 0, 0, tiled=True)
    incoming = incoming.reshape(HEAD_COUNT // 2, STATE, LANES)
    scaled_down = (down.astype(F32) * attn_norm_gain[None]).astype(BF)
    down_qkv = dot(scaled_down, weight.reshape(model, -1)).astype(BF)
    incoming, down_qkv = lax.optimization_barrier((incoming, down_qkv))

    encoded, main_in, sent_rows = scan_finish(
        yg,
        grown,
        bc,
        incoming,
        gate_norm_gain[None],
        mamba_out,
        byte_states,
        picked[None],
        down_proj,
    )
    columns = gather_columns(sent_rows, "sub")
    pieces = gather_rest(columns, "sub")
    main_up = dot(main_in, up_proj)
    groups = [pieces[: len(columns)], pieces[len(columns) :]]
    projected = []
    for group in groups:
        projected.append(project_qkv(down_qkv, group))
    keys = [kv for _, kv in projected]
    others = [partner(kv, "main") for kv in keys]
    far = []
    for kv in keys:
        far.append(far_shards(kv, "main"))
    q, stats, acc = near_attention(index, bias, [q for q, _ in projected], keys, others)
    stats, far = lax.optimization_barrier((stats, far))
    shards = []
    for k in range(mains // 2 - 1):
        direct = [group[k] for group in far]
        shards += [direct, [partner(part, "main") for part in direct]]
    heads_out = far_attention(index, q, stats, acc, bias, shards)
    own_heads = lax.all_to_all(heads_out.reshape(subs, CAP, heads * HD), "sub", 0, 0)
    span_up, edge_rows = project_up(index, main_up, own_heads, out_up, own_count)
    previous = lax.ppermute(edge_rows, axes, [(i, i + 1) for i in range(devices - 1)])[:2]
    table = jnp.concatenate([previous, span_up], 0)
    target = span_rank + 1
    spread = (target[:, None] == jnp.arange(CAP + 2)[None, :]).astype(BF)
    return (encoded.astype(F32) + dot(spread, table)).astype(BF)


def solution(mesh):
    return jax.shard_map(
        local,
        mesh=mesh,
        in_specs=(
            P(("main", "sub"), None),
            P(("main", "sub")),
            P(),
            P(),
            P(),
            P(),
            P(),
            P(),
            P(),
            P(),
            P(),
            P(),
            P(),
            P(),
            P(None, "sub", None),
            P("sub", None, None),
            P(),
        ),
        out_specs=P(("main", "sub"), None),
        check_vma=False,
    )
```

profile of v0, /device:TPU:5, one launch (start us, length us, event | category | flops | bytes accessed | tf_op | source)
XLA Modules:
  0.0 185.4 jit_solution(2574948549255607062)
XLA Ops:
  7.6 7.8 %scan_states.1 = (bf16[512,1024]{1,0:T(8,128)(2,1)}, bf16[512,2048]{1,0:T(8,128)(2,1)}, bf16[512,256]{1,0:T(8,128)(2,1)}, f32[512,128]{1,0:T(8,128)}, f32[512,12...) custom-call(bf16[512,1024]{1,0:T(8,128)(2,1)} %bytes_ref.1, f32[1,1024]{1,0:T(1,128)} %bitcast.48, ...), custom_call_target="tpu_custom_call" | custom-call | flops 5400000000 | bytes 27000000 | tf_op jit(solution)/shard_map/scan_states/pallas_call | solution.py:142
  15.8 7.0 %all-to-all-start = ((bf16[32,80,128]{2,1,0:T(8,128)(2,1)}), bf16[32,80,128]{2,1,0:T(8,128)(2,1)S(1)}, u32[]{:S(2)}, u32[]{:S(2)}) async-start(bf16[32,80,128]{2,1,0:T(8,128)(2,1)} %get-tuple-element.54), calls=%async_computation | async-start | bytes 1310720 | tf_op jit(solution)/shard_map/all_to_all | solution.py:705
  22.9 15.6 %scan_within.1 = (bf16[512,2048]{1,0:T(8,128)(2,1)}, bf16[512,2048]{1,0:T(8,128)(2,1)}) custom-call(bf16[512,1024]{1,0:T(8,128)(2,1)} %get-tuple-element.55.normed_ref, bf16[1024,4096]{1,0:T(8,128)(2,1)} %wg_ref.1, bf16[512,2048]{1,0:T(8,128)(2,1)} %get-tuple-element.56.x_ref, bf16[512,256]{1,0:T(8,128)(2,1)} %get-tuple-element.57.bc_ref.c_ref, ...), custom_call_target="tpu_custom_call" | custom-call | flops 8400000000 | bytes 42000000 | tf_op jit(solution)/shard_map/scan_within/pallas_call | solution.py:269
  43.2 9.9 %collective-permute-done.3 = bf16[1024,256]{1,0:T(8,128)(2,1)S(1)} collective-permute-done((bf16[1024,256]{1,0:T(8,128)(2,1)S(1)}, bf16[1024,256]{1,0:T(8,128)(2,1)S(1)}, u32[]{:S(2)}, u32[]{:S(2)}) %collective-permute-start.3) | collective-permute-done | bytes 524320 | tf_op jit(solution)/shard_map/ppermute | solution.py:386
  55.9 6.8 %all-to-all-start.1 = ((bf16[32,64,128]{2,1,0:T(8,128)(2,1)}), bf16[32,64,128]{2,1,0:T(8,128)(2,1)}, u32[]{:S(2)}, u32[]{:S(2)}) async-start(bf16[32,64,128]{2,1,0:T(8,128)(2,1)} %state_prefix.1), calls=%async_computation.1 | async-start | bytes 1048576 | tf_op jit(solution)/shard_map/all_to_all | solution.py:723
  62.8 2.7 %copy.21 = bf16[256,8,2,384]{3,1,2,0:T(8,128)(2,1)S(1)} copy(bf16[256,8,2,384]{3,2,1,0:T(2,128)(2,1)} %bitcast.39) | data formatting | bytes 6291456
  65.9 4.5 %fusion.2.weight_ref = bf16[1024,768]{1,0:T(8,128)(2,1)} fusion(bf16[2048,768]{1,0:T(8,128)(2,1)S(1)} %bitcast.40, bf16[1024,2048]{1,0:T(8,128)(2,1)S(1)} %copy-done.7, f32[2048]{0:T(1024)S(1)} %copy-done.13), kind=kOutput, calls=%fused_computation.5 | convolution fusion | flops 3228303360 | bytes 8921088 | tf_op jit(solution)/shard_map/dot_general | solution.py:33
  70.4 7.7 %all-to-all-done.1 = bf16[32,64,128]{2,1,0:T(8,128)(2,1)} async-done(((bf16[32,64,128]{2,1,0:T(8,128)(2,1)}), bf16[32,64,128]{2,1,0:T(8,128)(2,1)}, u32[]{:S(2)}, u32[]{:S(2)}) %all-to-all-start.1) | async-done | bytes 524320 | tf_op jit(solution)/shard_map/all_to_all | solution.py:723
  78.1 9.4 %scan_finish.1 = (bf16[512,1024]{1,0:T(8,128)(2,1)}, bf16[96,2048]{1,0:T(8,128)(2,1)}, bf16[96,1024]{1,0:T(8,128)(2,1)}) custom-call(bf16[512,2048]{1,0:T(8,128)(2,1)} %get-tuple-element.69.yg_ref, bf16[512,2048]{1,0:T(8,128)(2,1)} %get-tuple-element.70.grown_ref, bf16[512,256]{1,0:T(8,128)(2,1)} %get-tuple-element.57.bc_ref.c_ref, ...), custom_call_target="tpu_custom_call" | custom-call | flops 6000000000 | bytes 30000000 | tf_op jit(solution)/shard_map/scan_finish/pallas_call | solution.py:340
  91.1 4.9 %collective-permute-done.4.refs_1_ = bf16[96,1024]{1,0:T(8,128)(2,1)} collective-permute-done((bf16[96,1024]{1,0:T(8,128)(2,1)}, bf16[96,1024]{1,0:T(8,128)(2,1)}, u32[]{:S(2)}, u32[]{:S(2)}) %collective-permute-start.4) | collective-permute-done | bytes 196640 | tf_op jit(solution)/shard_map/ppermute | solution.py:386
  96.1 7.4 %collective-permute-done.5.refs_2_ = bf16[96,1024]{1,0:T(8,128)(2,1)} collective-permute-done((bf16[96,1024]{1,0:T(8,128)(2,1)}, bf16[96,1024]{1,0:T(8,128)(2,1)}, u32[]{:S(2)}, u32[]{:S(2)}) %collective-permute-start.5) | collective-permute-done | bytes 196640 | tf_op jit(solution)/shard_map/ppermute | solution.py:386
  104.9 3.5 %project_qkv.2 = (bf16[384,256]{1,0:T(8,128)(2,1)}, bf16[384,512]{1,0:T(8,128)(2,1)}) custom-call(bf16[1024,768]{1,0:T(8,128)(2,1)} %fusion.2.weight_ref, bf16[96,1024]{1,0:T(8,128)(2,1)} %get-tuple-element.82.refs_0_, bf16[96,1024]{1,0:T(8,128)(2,1)} %collective-permute-done.4.refs_1_, bf16[96,1024]{1,0:T(8,128)(2,1)} %collective-permute-done.5.refs_2_, ...), custom_call_target="tpu_custom_call" | custom-call | flops 2400000000 | bytes 12000000 | tf_op jit(solution)/shard_map/project_qkv/pallas_call | solution.py:448
  108.4 2.6 %collective-permute-start.11 = (bf16[384,512]{1,0:T(8,128)(2,1)}, bf16[384,512]{1,0:T(8,128)(2,1)}, u32[]{:S(2)}, u32[]{:S(2)}) collective-permute-start(bf16[384,512]{1,0:T(8,128)(2,1)} %get-tuple-element.85.refs_2_), channel_id=1, source_target_pairs={{0,8},{8,0},{16,24},{24,16},{1,9},{9,1},{17,25},{25,17},{2,10},{10... | collective-permute-start | bytes 1179656 | tf_op jit(solution)/shard_map/ppermute | solution.py:410
  112.5 3.5 %project_qkv.3 = (bf16[384,256]{1,0:T(8,128)(2,1)}, bf16[384,512]{1,0:T(8,128)(2,1)}) custom-call(bf16[1024,768]{1,0:T(8,128)(2,1)} %fusion.2.weight_ref, bf16[96,1024]{1,0:T(8,128)(2,1)} %copy-done.12, bf16[96,1024]{1,0:T(8,128)(2,1)} %collective-permute-done.8.refs_1_, bf16[96,1024]{1,0:T(8,128)(2,1)} %collective-permute-done.9.refs_2_, ...), custom_call_target="tpu_custom_call" | custom-call | flops 2400000000 | bytes 12000000 | tf_op jit(solution)/shard_map/project_qkv/pallas_call | solution.py:448
  115.9 2.9 %collective-permute-start.12 = (bf16[384,512]{1,0:T(8,128)(2,1)}, bf16[384,512]{1,0:T(8,128)(2,1)}, u32[]{:S(2)}, u32[]{:S(2)}) collective-permute-start(bf16[384,512]{1,0:T(8,128)(2,1)} %get-tuple-element.86.refs_3_), channel_id=1, source_target_pairs={{0,8},{8,0},{16,24},{24,16},{1,9},{9,1},{17,25},{25,17},{2,10},{10... | collective-permute-start | bytes 1179656 | tf_op jit(solution)/shard_map/ppermute | solution.py:410
  122.9 7.8 %near_attention.1 = (bf16[768,256]{1,0:T(8,128)(2,1)}, f32[4,768,128]{2,1,0:T(8,128)}, f32[768,256]{1,0:T(8,128)}) custom-call(s32[13]{0:T(128)} %stack.64.index_ref, f32[4,1,768]{2,1,0:T(1,128)} %compare_select_fusion.bias_ref, bf16[384,256]{1,0:T(8,128)(2,1)} %get-tuple-element.83.refs_0_, bf16[384,256]{1,0:T(8,128)(2,1)} %get-tuple-element.84.refs_1_, ...), custom_call_target="tpu_custom_call" | custom-call | flops 5400000000 | bytes 27000000 | tf_op jit(solution)/shard_map/near_attention/pallas_call | solution.py:579
  132.6 8.4 %collective-permute-done.14.refs_1_ = bf16[384,512]{1,0:T(8,128)(2,1)S(1)} collective-permute-done((bf16[384,512]{1,0:T(8,128)(2,1)}, bf16[384,512]{1,0:T(8,128)(2,1)S(1)}, u32[]{:S(2)}, u32[]{:S(2)}) %collective-permute-start.14) | collective-permute-done | bytes 393248 | tf_op jit(solution)/shard_map/ppermute | solution.py:654
  145.1 8.0 %far_attention.1 = bf16[768,256]{1,0:T(8,128)(2,1)} custom-call(s32[13]{0:T(128)} %stack.64.index_ref, bf16[768,256]{1,0:T(8,128)(2,1)} %get-tuple-element.87.q_ref, f32[4,768,128]{2,1,0:T(8,128)} %get-tuple-element.89.stats_in, f32[768,256]{1,0:T(8,128)} %get-tuple-element.90.acc_in, f32[4,1,768]{2,1,0:T(1,128)} %compare_select_fusion.bias_ref, ...), custom_call_target="tpu_custom_call" | custom-call | flops 5400000000 | bytes 27000000 | tf_op jit(solution)/shard_map/far_attention/pallas_call | solution.py:639
  153.1 5.3 %all-to-all-start.2 = ((bf16[8,96,256]{2,1,0:T(8,128)(2,1)}), bf16[8,96,256]{2,1,0:T(8,128)(2,1)S(1)}, u32[]{:S(2)}, u32[]{:S(2)}) async-start(bf16[8,96,256]{2,1,0:T(8,128)(2,1)} %bitcast.43), calls=%async_computation.2 | async-start | bytes 786432 | tf_op jit(solution)/shard_map/all_to_all | solution.py:759
  158.3 3.8 %fusion.15.main_up_ref = f32[96,1024]{1,0:T(8,128)} fusion(bf16[96,2048]{1,0:T(8,128)(2,1)S(1)} %copy-done.3, bf16[2048,1024]{1,0:T(8,128)(2,1)} %param.33), kind=kOutput, calls=%fused_computation.33 | convolution fusion | flops 402653184 | bytes 4980736 | tf_op jit(solution)/shard_map/dot_general | solution.py:33
  162.1 7.3 %all-to-all-done.2.heads_ref = bf16[8,96,256]{2,1,0:T(8,128)(2,1)S(1)} async-done(((bf16[8,96,256]{2,1,0:T(8,128)(2,1)}), bf16[8,96,256]{2,1,0:T(8,128)(2,1)S(1)}, u32[]{:S(2)}, u32[]{:S(2)}) %all-to-all-start.2) | async-done | bytes 393248 | tf_op jit(solution)/shard_map/all_to_all | solution.py:759
  170.2 4.7 %project_up.1 = (bf16[96,1024]{1,0:T(8,128)(2,1)}, bf16[16,1024]{1,0:T(8,128)(2,1)}) custom-call(s32[13]{0:T(128)} %stack.64.index_ref, s32[1]{0:T(128)} %bitcast.22.edge_ref, f32[96,1024]{1,0:T(8,128)} %fusion.15.main_up_ref, bf16[8,96,256]{2,1,0:T(8,128)(2,1)} %copy-done.4, bf16[2,2048,256]{2,1,0:T(8,128)(2,1)} %pad_maximum_fusion.own_ref, ...), custom_call_target="tpu_custom_call" | custom-call | flops 3000000000 | bytes 15000000 | tf_op jit(solution)/shard_map/project_up/pallas_call | solution.py:492
  174.9 3.2 %collective-permute-start.19 = (bf16[16,1024]{1,0:T(8,128)(2,1)}, bf16[16,1024]{1,0:T(8,128)(2,1)S(1)}, u32[]{:S(2)}, u32[]{:S(2)}) collective-permute-start(bf16[16,1024]{1,0:T(8,128)(2,1)} %get-tuple-element.95), channel_id=1, source_target_pairs={{0,1},{1,2},{2,3},{3,4},{4,5},{5,6},{6,7},{7,8},{8,9},{9,10},{10,1... | collective-permute-start | bytes 98312 | tf_op jit(solution)/shard_map/ppermute | solution.py:761
  178.1 4.9 %collective-permute-done.19 = bf16[16,1024]{1,0:T(8,128)(2,1)S(1)} collective-permute-done((bf16[16,1024]{1,0:T(8,128)(2,1)}, bf16[16,1024]{1,0:T(8,128)(2,1)S(1)}, u32[]{:S(2)}, u32[]{:S(2)}) %collective-permute-start.19) | collective-permute-done | bytes 32800 | tf_op jit(solution)/shard_map/ppermute | solution.py:761
  (84 shorter events, 35.8 us)
Async XLA Ops:
  2.9 12.6 %collective-permute-start = (bf16[256,256]{1,0:T(8,128)(2,1)S(1)}, bf16[256,256]{1,0:T(8,128)(2,1)S(1)}, u32[]{:S(2)}, u32[]{:S(2)}) collective-permute-start(bf16[256,256]{1,0:T(8,128)(2,1)S(1)} %fusion.3), channel_id=1, source_target_pairs={{0,2},{1,3},{2,4},{3,5},{4,6},{5,7},{6,0},{7,1},{8,10},{9,11},{10,... | collective-permute-start | bytes 393224 | tf_op jit(solution)/shard_map/ppermute | solution.py:386
  4.2 11.6 %collective-permute-start.1 = (bf16[256,256]{1,0:T(8,128)(2,1)S(1)}, bf16[256,256]{1,0:T(8,128)(2,1)S(1)}, u32[]{:S(2)}, u32[]{:S(2)}) collective-permute-start(bf16[256,256]{1,0:T(8,128)(2,1)S(1)} %fusion.3), channel_id=1, source_target_pairs={{0,4},{1,5},{2,6},{3,7},{4,0},{5,1},{6,2},{7,3},{8,12},{9,13},{10,... | collective-permute-start | bytes 393224 | tf_op jit(solution)/shard_map/ppermute | solution.py:386
  6.6 9.3 %collective-permute-start.2 = (bf16[256,256]{1,0:T(8,128)(2,1)S(1)}, bf16[256,256]{1,0:T(8,128)(2,1)S(1)}, u32[]{:S(2)}, u32[]{:S(2)}) collective-permute-start(bf16[256,256]{1,0:T(8,128)(2,1)S(1)} %fusion.3), channel_id=1, source_target_pairs={{0,6},{1,7},{2,0},{3,1},{4,2},{5,3},{6,4},{7,5},{8,14},{9,15},{10,... | collective-permute-start | bytes 393224 | tf_op jit(solution)/shard_map/ppermute | solution.py:386
  15.8 37.2 %all-to-all-start = ((bf16[32,80,128]{2,1,0:T(8,128)(2,1)}), bf16[32,80,128]{2,1,0:T(8,128)(2,1)S(1)}, u32[]{:S(2)}, u32[]{:S(2)}) async-start(bf16[32,80,128]{2,1,0:T(8,128)(2,1)} %get-tuple-element.54), calls=%async_computation | async-start | bytes 1310720 | tf_op jit(solution)/shard_map/all_to_all | solution.py:705
  39.9 13.2 %collective-permute-start.3 = (bf16[1024,256]{1,0:T(8,128)(2,1)S(1)}, bf16[1024,256]{1,0:T(8,128)(2,1)S(1)}, u32[]{:S(2)}, u32[]{:S(2)}) collective-permute-start(bf16[1024,256]{1,0:T(8,128)(2,1)S(1)} %constant_dynamic-update-slice_fusion), channel_id=1, source_target_pairs={{0,1},{1,0},{2,3},{3,2},{4,5},{5,4},{6,7},{7,6},{8,9},{9,8},{10,11... | collective-permute-start | bytes 1572872 | tf_op jit(solution)/shard_map/ppermute | solution.py:386
  55.9 22.1 %all-to-all-start.1 = ((bf16[32,64,128]{2,1,0:T(8,128)(2,1)}), bf16[32,64,128]{2,1,0:T(8,128)(2,1)}, u32[]{:S(2)}, u32[]{:S(2)}) async-start(bf16[32,64,128]{2,1,0:T(8,128)(2,1)} %state_prefix.1), calls=%async_computation.1 | async-start | bytes 1048576 | tf_op jit(solution)/shard_map/all_to_all | solution.py:723
  65.5 53.3 %collective-permute-start.17 = (bf16[2048,256]{1,0:T(8,128)(2,1)S(1)}, bf16[2048,256]{1,0:T(8,128)(2,1)S(1)}, u32[]{:S(2)}, u32[]{:S(2)}) collective-permute-start(bf16[2048,256]{1,0:T(8,128)(2,1)S(1)} %constant_dynamic-update-slice_fusion.4), channel_id=1, source_target_pairs={{0,16},{8,24},{16,0},{24,8},{1,17},{9,25},{17,1},{25,9},{2,18},{10... | collective-permute-start | bytes 3145736 | tf_op jit(solution)/shard_map/ppermute | solution.py:416
  87.4 8.6 %collective-permute-start.4 = (bf16[96,1024]{1,0:T(8,128)(2,1)}, bf16[96,1024]{1,0:T(8,128)(2,1)}, u32[]{:S(2)}, u32[]{:S(2)}) collective-permute-start(bf16[96,1024]{1,0:T(8,128)(2,1)} %get-tuple-element.82.refs_0_), channel_id=1, source_target_pairs={{0,2},{1,3},{2,4},{3,5},{4,6},{5,7},{6,0},{7,1},{8,10},{9,11},{10,... | collective-permute-start | bytes 589832 | tf_op jit(solution)/shard_map/ppermute | solution.py:386
  87.7 15.8 %collective-permute-start.5 = (bf16[96,1024]{1,0:T(8,128)(2,1)}, bf16[96,1024]{1,0:T(8,128)(2,1)}, u32[]{:S(2)}, u32[]{:S(2)}) collective-permute-start(bf16[96,1024]{1,0:T(8,128)(2,1)} %get-tuple-element.82.refs_0_), channel_id=1, source_target_pairs={{0,4},{1,5},{2,6},{3,7},{4,0},{5,1},{6,2},{7,3},{8,12},{9,13},{10,... | collective-permute-start | bytes 589832 | tf_op jit(solution)/shard_map/ppermute | solution.py:386
  89.1 14.5 %collective-permute-start.6 = (bf16[96,1024]{1,0:T(8,128)(2,1)}, bf16[96,1024]{1,0:T(8,128)(2,1)}, u32[]{:S(2)}, u32[]{:S(2)}) collective-permute-start(bf16[96,1024]{1,0:T(8,128)(2,1)} %get-tuple-element.82.refs_0_), channel_id=1, source_target_pairs={{0,6},{1,7},{2,0},{3,1},{4,2},{5,3},{6,4},{7,5},{8,14},{9,15},{10,... | collective-permute-start | bytes 589832 | tf_op jit(solution)/shard_map/ppermute | solution.py:386
  90.7 17.7 %collective-permute-start.7 = (bf16[96,1024]{1,0:T(8,128)(2,1)}, bf16[96,1024]{1,0:T(8,128)(2,1)S(1)}, u32[]{:S(2)}, u32[]{:S(2)}) collective-permute-start(bf16[96,1024]{1,0:T(8,128)(2,1)} %get-tuple-element.82.refs_0_), channel_id=1, source_target_pairs={{0,1},{1,0},{2,3},{3,2},{4,5},{5,4},{6,7},{7,6},{8,9},{9,8},{10,11... | collective-permute-start | bytes 589832 | tf_op jit(solution)/shard_map/ppermute | solution.py:386
  96.1 15.0 %collective-permute-start.8 = (bf16[96,1024]{1,0:T(8,128)(2,1)}, bf16[96,1024]{1,0:T(8,128)(2,1)}, u32[]{:S(2)}, u32[]{:S(2)}) collective-permute-start(bf16[96,1024]{1,0:T(8,128)(2,1)} %collective-permute-done.4.refs_1_), channel_id=1, source_target_pairs={{0,1},{1,0},{2,3},{3,2},{4,5},{5,4},{6,7},{7,6},{8,9},{9,8},{10,11... | collective-permute-start | bytes 589832 | tf_op jit(solution)/shard_map/ppermute | solution.py:386
  103.5 7.6 %collective-permute-start.9 = (bf16[96,1024]{1,0:T(8,128)(2,1)}, bf16[96,1024]{1,0:T(8,128)(2,1)}, u32[]{:S(2)}, u32[]{:S(2)}) collective-permute-start(bf16[96,1024]{1,0:T(8,128)(2,1)} %collective-permute-done.5.refs_2_), channel_id=1, source_target_pairs={{0,1},{1,0},{2,3},{3,2},{4,5},{5,4},{6,7},{7,6},{8,9},{9,8},{10,11... | collective-permute-start | bytes 589832 | tf_op jit(solution)/shard_map/ppermute | solution.py:386
  103.6 8.8 %collective-permute-start.10 = (bf16[96,1024]{1,0:T(8,128)(2,1)}, bf16[96,1024]{1,0:T(8,128)(2,1)}, u32[]{:S(2)}, u32[]{:S(2)}) collective-permute-start(bf16[96,1024]{1,0:T(8,128)(2,1)} %collective-permute-done.6.refs_3_), channel_id=1, source_target_pairs={{0,1},{1,0},{2,3},{3,2},{4,5},{5,4},{6,7},{7,6},{8,9},{9,8},{10,11... | collective-permute-start | bytes 589832 | tf_op jit(solution)/shard_map/ppermute | solution.py:386
  108.4 14.5 %collective-permute-start.11 = (bf16[384,512]{1,0:T(8,128)(2,1)}, bf16[384,512]{1,0:T(8,128)(2,1)}, u32[]{:S(2)}, u32[]{:S(2)}) collective-permute-start(bf16[384,512]{1,0:T(8,128)(2,1)} %get-tuple-element.85.refs_2_), channel_id=1, source_target_pairs={{0,8},{8,0},{16,24},{24,16},{1,9},{9,1},{17,25},{25,17},{2,10},{10... | collective-permute-start | bytes 1179656 | tf_op jit(solution)/shard_map/ppermute | solution.py:410
  115.9 7.0 %collective-permute-start.12 = (bf16[384,512]{1,0:T(8,128)(2,1)}, bf16[384,512]{1,0:T(8,128)(2,1)}, u32[]{:S(2)}, u32[]{:S(2)}) collective-permute-start(bf16[384,512]{1,0:T(8,128)(2,1)} %get-tuple-element.86.refs_3_), channel_id=1, source_target_pairs={{0,8},{8,0},{16,24},{24,16},{1,9},{9,1},{17,25},{25,17},{2,10},{10... | collective-permute-start | bytes 1179656 | tf_op jit(solution)/shard_map/ppermute | solution.py:410
  120.3 49.1 %collective-permute-start.18 = (bf16[2,2048,256]{2,1,0:T(8,128)(2,1)}, bf16[2,2048,256]{2,1,0:T(8,128)(2,1)}, u32[]{:S(2)}, u32[]{:S(2)}) collective-permute-start(bf16[2,2048,256]{2,1,0:T(8,128)(2,1)} %pad_maximum_fusion.own_ref), channel_id=1, source_target_pairs={{0,8},{8,0},{16,24},{24,16},{1,9},{9,1},{17,25},{25,17},{2,10},{10... | collective-permute-start | bytes 6291464 | tf_op jit(solution)/shard_map/ppermute | solution.py:410
  120.3 12.3 %collective-permute-start.13 = (bf16[384,512]{1,0:T(8,128)(2,1)}, bf16[384,512]{1,0:T(8,128)(2,1)S(1)}, u32[]{:S(2)}, u32[]{:S(2)}) collective-permute-start(bf16[384,512]{1,0:T(8,128)(2,1)} %get-tuple-element.85.refs_2_), channel_id=1, source_target_pairs={{0,16},{8,24},{1,17},{9,25},{2,18},{10,26},{3,19},{11,27},{4,20},{... | collective-permute-start | bytes 1179656 | tf_op jit(solution)/shard_map/ppermute | solution.py:654
  121.6 19.4 %collective-permute-start.14 = (bf16[384,512]{1,0:T(8,128)(2,1)}, bf16[384,512]{1,0:T(8,128)(2,1)S(1)}, u32[]{:S(2)}, u32[]{:S(2)}) collective-permute-start(bf16[384,512]{1,0:T(8,128)(2,1)} %get-tuple-element.86.refs_3_), channel_id=1, source_target_pairs={{0,16},{8,24},{1,17},{9,25},{2,18},{10,26},{3,19},{11,27},{4,20},{... | collective-permute-start | bytes 1179656 | tf_op jit(solution)/shard_map/ppermute | solution.py:654
  141.0 2.7 %collective-permute-start.15 = (bf16[384,512]{1,0:T(8,128)(2,1)S(1)}, bf16[384,512]{1,0:T(8,128)(2,1)S(1)}, u32[]{:S(2)}, u32[]{:S(2)}) collective-permute-start(bf16[384,512]{1,0:T(8,128)(2,1)S(1)} %collective-permute-done.13.refs_0_), channel_id=1, source_target_pairs={{0,8},{8,0},{16,24},{24,16},{1,9},{9,1},{17,25},{25,17},{2,10},{10... | collective-permute-start | bytes 1179656 | tf_op jit(solution)/shard_map/ppermute | solution.py:410
  142.4 1.9 %collective-permute-start.16 = (bf16[384,512]{1,0:T(8,128)(2,1)S(1)}, bf16[384,512]{1,0:T(8,128)(2,1)S(1)}, u32[]{:S(2)}, u32[]{:S(2)}) collective-permute-start(bf16[384,512]{1,0:T(8,128)(2,1)S(1)} %collective-permute-done.14.refs_1_), channel_id=1, source_target_pairs={{0,8},{8,0},{16,24},{24,16},{1,9},{9,1},{17,25},{25,17},{2,10},{10... | collective-permute-start | bytes 1179656 | tf_op jit(solution)/shard_map/ppermute | solution.py:410
  153.1 16.4 %all-to-all-start.2 = ((bf16[8,96,256]{2,1,0:T(8,128)(2,1)}), bf16[8,96,256]{2,1,0:T(8,128)(2,1)S(1)}, u32[]{:S(2)}, u32[]{:S(2)}) async-start(bf16[8,96,256]{2,1,0:T(8,128)(2,1)} %bitcast.43), calls=%async_computation.2 | async-start | bytes 786432 | tf_op jit(solution)/shard_map/all_to_all | solution.py:759
  162.1 20.9 %copy-start.1 = (bf16[512,1024]{1,0:T(8,128)(2,1)S(1)}, bf16[512,1024]{1,0:T(8,128)(2,1)}, u32[]{:S(2)}) copy-start(bf16[512,1024]{1,0:T(8,128)(2,1)} %get-tuple-element.76) | copy-start | bytes 3145732
  174.9 8.1 %collective-permute-start.19 = (bf16[16,1024]{1,0:T(8,128)(2,1)}, bf16[16,1024]{1,0:T(8,128)(2,1)S(1)}, u32[]{:S(2)}, u32[]{:S(2)}) collective-permute-start(bf16[16,1024]{1,0:T(8,128)(2,1)} %get-tuple-element.95), channel_id=1, source_target_pairs={{0,1},{1,2},{2,3},{3,4},{4,5},{5,6},{6,7},{7,8},{8,9},{9,10},{10,1... | collective-permute-start | bytes 98312 | tf_op jit(solution)/shard_map/ppermute | solution.py:761
  (13 other events, 75.7 us)
where the time goes:
time: 188 us; the launch traced here: 185 us
  Pallas kernels  62.2 us (33%)
  waiting for transfers between devices  56.2 us (30%)
  starting transfers between devices  43 us (23%)
  matrix products  12.3 us (7%)
  local copies, waits for them, and re-layouts  7.71 us (4%)
  other arithmetic  3.81 us (2%)
    ppermute x11, waiting for transfers between devices, sub_move(): return lax.ppermute(value, axis, route)  24 us
    pallas_call x1, Pallas kernels, scan_within(): pl.pallas_call(within_body, grid=(steps,), in_specs=[whole((rows, width))...  15.6 us
    dot_general x4, matrix products, dot(): return jnp.dot(a, b, preferred_element_type=F32, **kw)  12.3 us
    ppermute x11, starting transfers between devices, sub_move(): return lax.ppermute(value, axis, route)  11.1 us
    ppermute x2, waiting for transfers between devices, far_shards(): lax.ppermute(kv, axis, [(i - k, i) for i in range(k, count)])  10.3 us
    pallas_call x1, Pallas kernels, scan_finish(): pl.pallas_call(finish_body, grid=(steps,), in_specs=[pl.BlockSpec((rows,...  9.35 us
    pallas_call x1, Pallas kernels, far_attention(): pl.pallas_call(functools.partial(far_body, shards=len(shards)), in_specs=...  8 us
    pallas_call x1, Pallas kernels, scan_states(): pl.pallas_call(states_body, grid=(steps,), in_specs=[whole((rows, width))...  7.82 us
  transfers between devices with their start and end apart: 23, of which 12 were waited for; matrix products, arithmetic and copies ran while one was open for 9% of the time, Pallas kernels for 30%

commit v1 on v0

--- a/solution.py
+++ b/solution.py
@@ -17,7 +17,7 @@
 CAP = 96
 CHUNK = 128
 LANES = 128
-QUAD = 256
+WITHIN_STEP = 512
 STATE_STEP = 1024
 FINISH_STEP = 1024
 EXTRA = 16
@@ -224,11 +224,11 @@
             bt_ref[c] = bc_ref[at, :STATE].astype(F32).T.astype(BF)
 
     gate = silu(dot(normed_ref[...], wg_ref[...]))
-    cum = step_columns(cum_ref[...], j, QUAD)
-    chunk = step_columns(chunk_ref[...], j, QUAD)
-    skip = step_columns(jnp.broadcast_to(padded(skip_ref), (8, LANES)), j, QUAD)
+    cum = step_columns(cum_ref[...], j, WITHIN_STEP)
+    chunk = step_columns(chunk_ref[...], j, WITHIN_STEP)
+    skip = step_columns(jnp.broadcast_to(padded(skip_ref), (8, LANES)), j, WITHIN_STEP)
     lane = lax.broadcasted_iota(jnp.int32, (CHUNK, LANES), 1)
-    for pair in range(2):
+    for pair in range(WITHIN_STEP // LANES):
         lanes = slice(pair * LANES, (pair + 1) * LANES)
         skips = pair_lanes(skip, pair)[:1]
         end = jnp.zeros((1, LANES), F32)
@@ -238,7 +238,7 @@
             part = slice(c * CHUNK, (c + 1) * CHUNK)
             weights = []
             for head in (2 * pair, 2 * pair + 1):
-                gap = cum[part, head : head + 1] - late_ref[0, head : head + 1, at]
+                gap = cum[part, head : head + 1] - late_ref[head // 4, head % 4 : head % 4 + 1, at]
                 weights.append((jnp.exp2(jnp.minimum(gap, 126.0)) * contact_ref[c]).astype(BF))
             packed = x_ref[at, lanes]
             zero = jnp.zeros_like(packed)
@@ -265,21 +265,21 @@
 def scan_within(normed, mamba_in, x, bc, cum, chunk, late, skip):
     rows, width = normed.shape
     chunks = rows // CHUNK
-    steps = INNER_WIDTH // QUAD
+    steps = INNER_WIDTH // WITHIN_STEP
     return pl.pallas_call(
         within_body,
         grid=(steps,),
         in_specs=[
             whole((rows, width)),
-            pl.BlockSpec((width, QUAD), lambda j: (0, j + steps)),
-            pl.BlockSpec((rows, QUAD), lambda j: (0, j)),
+            pl.BlockSpec((width, WITHIN_STEP), lambda j: (0, j + steps)),
+            pl.BlockSpec((rows, WITHIN_STEP), lambda j: (0, j)),
             whole((rows, 2 * STATE)),
             whole((rows, LANES)),
             whole((rows, LANES)),
-            pl.BlockSpec((1, 8, rows), lambda j: (j, 0, 0)),
+            pl.BlockSpec((WITHIN_STEP // 256, 8, rows), lambda j: (j, 0, 0)),
             whole((1, HEAD_COUNT)),
         ],
-        out_specs=[pl.BlockSpec((rows, QUAD), lambda j: (0, j))] * 2,
+        out_specs=[pl.BlockSpec((rows, WITHIN_STEP), lambda j: (0, j))] * 2,
         out_shape=[jax.ShapeDtypeStruct((rows, INNER_WIDTH), BF)] * 2,
         scratch_shapes=[
             pltpu.VMEM((chunks, CHUNK, CHUNK), F32),
@@ -386,14 +386,23 @@
     return lax.ppermute(value, axis, route)
 
 
+def places(major):
+    return [0, 1, major - 1] + list(range(2, major - 1))
+
+
 def gather_columns(block, axis):
     major, _ = sub_grid(lax.axis_size(axis))
-    return [block] + [sub_move(block, axis, dz, 0) for dz in range(1, major)]
+    return [block] + [sub_move(block, axis, dz, 0) for dz in places(major)[1:]]
+
+
+def forward(value, axis):
+    _, minor = sub_grid(lax.axis_size(axis))
+    return [sub_move(value, axis, 0, dx) for dx in range(1, minor)]
 
 
 def gather_rest(columns, axis):
-    _, minor = sub_grid(lax.axis_size(axis))
-    return columns + [sub_move(c, axis, 0, dx) for dx in range(1, minor) for c in columns]
+    moved = [forward(c, axis) for c in columns]
+    return columns + [piece for dx in zip(*moved) for piece in dx]
 
 
 def sub_sources(axis):
@@ -402,7 +411,7 @@
     me = lax.axis_index(axis)
     z, x = me // minor, me % minor
     return [(z - dz) % major * minor + (x - dx) % minor
-            for dx in range(minor) for dz in range(major)]
+            for dx in range(minor) for dz in places(major)]
 
 
 def partner(value, axis):
@@ -416,8 +425,7 @@
         lax.ppermute(block, axis, [(i, (i + k) % count) for i in range(count)])
         for k in range(2, count, 2)
     ]
-    near = jnp.stack(near)
-    return near, partner(near, axis)
+    return near + [partner(part, axis) for part in near]
 
 
 def main_sources(axis):
@@ -467,16 +475,17 @@
             first += 1
 
 
-def span_up_body(
-    index_ref, edge_ref, main_up_ref, heads_ref, own_ref, other_ref, up_ref, edges_ref, columns_ref
-):
+def span_up_body(index_ref, edge_ref, main_up_ref, heads_ref, *refs):
+    *weights, up_ref, edges_ref, columns_ref = refs
     subs, cap, _ = heads_ref.shape
-    half = own_ref.shape[0]
-    mains = 2 * half
+    mains = columns_ref.shape[0]
+    depth = weights[0].shape[0]
     flat = jnp.concatenate([heads_ref[index_ref[1 + mains + r]] for r in range(subs)], 1)
-    for p in range(half):
-        columns_ref[index_ref[1 + p]] = dot(flat, own_ref[p])
-        columns_ref[index_ref[1 + half + p]] = dot(flat, other_ref[p])
+    for p in range(mains):
+        part = 0.0
+        for g, weight in enumerate(weights[p::mains]):
+            part = part + dot(flat[:, g * depth : (g + 1) * depth], weight[...])
+        columns_ref[index_ref[1 + p]] = part
     joined = jnp.concatenate([columns_ref[p] for p in range(mains)], 1)
     up = (main_up_ref[...] + joined).astype(BF)
     up_ref[...] = up
@@ -486,24 +495,25 @@
     edges_ref[...] = dot(picker, up).astype(BF)
 
 
-def project_up(index, main_up, heads, weights, own_count):
+def project_up(index, main_up, heads, groups, own_count):
     cap, width = main_up.shape
-    half, _, part = weights[0].shape
+    part = groups[0][0].shape[1]
+    weights = [weight for group in groups for weight in group]
     return pl.pallas_call(
         span_up_body,
-        in_specs=[SCALARS, SCALARS] + vmem(4),
+        in_specs=[SCALARS, SCALARS] + vmem(2 + len(weights)),
         out_specs=vmem(2),
         out_shape=[
             jax.ShapeDtypeStruct((cap, width), BF),
             jax.ShapeDtypeStruct((16, width), BF),
         ],
-        scratch_shapes=[pltpu.VMEM((2 * half, cap, part), F32)],
+        scratch_shapes=[pltpu.VMEM((len(groups[0]), cap, part), F32)],
         cost_estimate=cost(5),
         name="project_up",
     )(index, own_count, main_up, heads, *weights)
 
 
-BLOCK = 256
+BLOCK = 384
 
 
 def scores_of(q, kv_ref, bias, head, span):
@@ -682,12 +692,6 @@
     heads = qkv_weight.shape[1]
     model = qkv_weight.shape[0]
 
-    up_part = width // mains
-    up_columns = lax.dynamic_slice_in_dim(up_proj, main_id * up_part, up_part, 1)
-    out_up = dot(out_weight.reshape(heads * HD, model), up_columns).astype(BF)
-    out_up, byte_states = lax.optimization_barrier((out_up, byte_states))
-    out_up = gather_columns(out_up, "sub")
-
     normed, x, bc, cum, chunk, late, send = scan_states(
         byte_states,
         enc_norm_gain[None],
@@ -698,33 +702,28 @@
         decay_rate[None],
         devices,
     )
-    send, flags, counts, *out_up = lax.optimization_barrier(
-        (send, boundary_flags, span_counts, *out_up)
+    send, weight, up, out, main_id = lax.optimization_barrier(
+        (send, qkv_weight, up_proj, out_weight, main_id)
     )
-    out_up = gather_rest([jnp.concatenate(out_up, 0)], "sub")
     parts = lax.all_to_all(send, axes, 0, 0, tiled=True)
+    weight = weight.reshape(model, -1)
+    up_part = width // mains
+    up_columns = lax.dynamic_slice_in_dim(up, main_id * up_part, up_part, 1)
+    out_up = dot(out.reshape(heads * HD, model), up_columns).astype(BF)
     yg, grown = scan_within(normed, mamba_in, x, bc, cum, chunk, late, skip_gain[None])
-    sub_index = sub_sources("sub")
-    index = jnp.stack([main_id] + main_sources("main") + sub_index).astype(jnp.int32)
-    slot = jnp.arange(subs * CAP, dtype=jnp.int32)
-    valid = slot[None] % CAP < jnp.repeat(counts.reshape(mains, subs), CAP, axis=1)
-    bias = jnp.where(valid, 0.0, -1e30).astype(F32)[:, None, :]
-    span_rank = jnp.cumsum(flags) - 1
-    picked = jnp.where(flags == 1, span_rank, -1)
-    device_ids = jnp.arange(devices, dtype=jnp.int32)
-    device_id = main_id * subs + lax.axis_index("sub")
-    own_count = jnp.sum(jnp.where(device_ids == device_id, counts, 0))[None]
-    parts, yg, grown, index, bias, picked, own_count, down, weight, *out_up = (
-        lax.optimization_barrier(
-            (parts, yg, grown, index, bias, picked, own_count, down_proj, qkv_weight, *out_up)
-        )
+    parts, yg, grown, down, weight, flags, out_up = lax.optimization_barrier(
+        (parts, yg, grown, down_proj, weight, boundary_flags, out_up)
     )
-    out_up = gather_main(jnp.concatenate(out_up, 0), "main")
     incoming = lax.all_to_all(state_prefix(parts), axes, 0, 0, tiled=True)
     incoming = incoming.reshape(HEAD_COUNT // 2, STATE, LANES)
     scaled_down = (down.astype(F32) * attn_norm_gain[None]).astype(BF)
-    down_qkv = dot(scaled_down, weight.reshape(model, -1)).astype(BF)
-    incoming, down_qkv = lax.optimization_barrier((incoming, down_qkv))
+    down_qkv = dot(scaled_down, weight).astype(BF)
+    span_rank = jnp.cumsum(flags) - 1
+    picked = jnp.where(flags == 1, span_rank, -1)
+    incoming, down_qkv, picked, out_up = lax.optimization_barrier(
+        (incoming, down_qkv, picked, out_up)
+    )
+    out_up = gather_columns(out_up, "sub")
 
     encoded, main_in, sent_rows = scan_finish(
         yg,
@@ -737,7 +736,21 @@
         picked[None],
         down_proj,
     )
+    sent_rows, counts, main_id, *out_up = lax.optimization_barrier(
+        (sent_rows, span_counts, main_id, *out_up)
+    )
+    out_up = jnp.concatenate(out_up, 0)
+    out_ups = [gather_main(out_up, "main")]
     columns = gather_columns(sent_rows, "sub")
+    sub_index = sub_sources("sub")
+    index = jnp.stack([main_id] + main_sources("main") + sub_index).astype(jnp.int32)
+    slot = jnp.arange(subs * CAP, dtype=jnp.int32)
+    valid = slot[None] % CAP < jnp.repeat(counts.reshape(mains, subs), CAP, axis=1)
+    bias = jnp.where(valid, 0.0, -1e30).astype(F32)[:, None, :]
+    device_ids = jnp.arange(devices, dtype=jnp.int32)
+    device_id = main_id * subs + lax.axis_index("sub")
+    own_count = jnp.sum(jnp.where(device_ids == device_id, counts, 0))[None]
+    columns[1], index, bias = lax.optimization_barrier((columns[1], index, bias))
     pieces = gather_rest(columns, "sub")
     main_up = dot(main_in, up_proj)
     groups = [pieces[: len(columns)], pieces[len(columns) :]]
@@ -745,24 +758,30 @@
     for group in groups:
         projected.append(project_qkv(down_qkv, group))
     keys = [kv for _, kv in projected]
+    keys[-1], out_up = lax.optimization_barrier((keys[-1], out_up))
+    out_up = forward(out_up, "sub")
     others = [partner(kv, "main") for kv in keys]
     far = []
     for kv in keys:
         far.append(far_shards(kv, "main"))
     q, stats, acc = near_attention(index, bias, [q for q, _ in projected], keys, others)
-    stats, far = lax.optimization_barrier((stats, far))
+    stats, far, *out_up = lax.optimization_barrier((stats, far, *out_up))
+    out_ups += [gather_main(part, "main") for part in out_up]
     shards = []
     for k in range(mains // 2 - 1):
         direct = [group[k] for group in far]
         shards += [direct, [partner(part, "main") for part in direct]]
     heads_out = far_attention(index, q, stats, acc, bias, shards)
     own_heads = lax.all_to_all(heads_out.reshape(subs, CAP, heads * HD), "sub", 0, 0)
-    span_up, edge_rows = project_up(index, main_up, own_heads, out_up, own_count)
-    previous = lax.ppermute(edge_rows, axes, [(i, i + 1) for i in range(devices - 1)])[:2]
-    table = jnp.concatenate([previous, span_up], 0)
-    target = span_rank + 1
-    spread = (target[:, None] == jnp.arange(CAP + 2)[None, :]).astype(BF)
-    return (encoded.astype(F32) + dot(spread, table)).astype(BF)
+    span_up, edge_rows = project_up(index, main_up, own_heads, out_ups, own_count)
+    previous = lax.ppermute(edge_rows, axes, [(i, i + 1) for i in range(devices - 1)])
+    target = span_rank - 1
+    spread = (target[:, None] == jnp.arange(CAP)[None, :]).astype(BF)
+    inner = (encoded.astype(F32) + dot(spread, span_up)).astype(BF)
+    inner, previous = lax.optimization_barrier((inner, previous))
+    before = jnp.where((target == -1)[:, None], previous[1][None], previous[0][None])
+    outer = (encoded.astype(F32) + before.astype(F32)).astype(BF)
+    return jnp.where((target < 0)[:, None], outer, inner)
 
 
 def solution(mesh):

time: 188 us -> 172 us (0.915)
  waiting for transfers between devices: 56.2 us -> 46.9 us
  starting transfers between devices: 43 us -> 37.9 us
  Pallas kernels: 62.2 us -> 58.1 us
  matrix products: 12.3 us -> 14.6 us
    ppermute x1 -> x2, waiting for transfers between devices: 0.01 us -> 8.18 us  [gather_main(): lax.ppermute(block, axis, [(i, (i + k) % count) for i in range(count)])]
    all_to_all x1, waiting for transfers between devices: 7.33 us -> 0.01 us  [local(): lax.all_to_all(heads_out.reshape(subs, CAP, heads * HD), 'sub', 0, 0)]
    ppermute x11, waiting for transfers between devices: 24 us -> 17.5 us  [sub_move(): return lax.ppermute(value, axis, route)]
    ppermute x11, starting transfers between devices: 11.1 us -> 8.16 us  [sub_move(): return lax.ppermute(value, axis, route)]
    pallas_call x1, Pallas kernels: 15.6 us -> 13 us  [scan_within(): pl.pallas_call(within_body, grid=(steps,), in_specs=[whole((rows, width))...]
    dot_general x4, matrix products: 12.3 us -> 14.6 us  [dot(): return jnp.dot(a, b, preferred_element_type=F32, **kw)]
    unnamed x33 -> x46, local copies, waits for them, and re-layouts: 6.55 us -> 7.72 us
    ppermute x5 -> x8, starting transfers between devices: 6.85 us -> 5.93 us  [partner(): return lax.ppermute(value, axis, [(i, i ^ 1) for i in range(count)])]
  transfers between devices with their start and end apart: 23 -> 27, of which waited for: 12 -> 11; matrix products, arithmetic and copies ran while one was open for 9% -> 13% of each run, Pallas kernels for 30% -> 25%
where the time goes in v1:
time: 172 us; the launch traced here: 171 us
  Pallas kernels  58.1 us (34%)
  waiting for transfers between devices  46.9 us (27%)
  starting transfers between devices  37.9 us (22%)
  matrix products  14.6 us (8%)
  local copies, waits for them, and re-layouts  8.91 us (5%)
  other arithmetic  3.79 us (2%)
    ppermute x11, waiting for transfers between devices, sub_move(): return lax.ppermute(value, axis, route)  17.5 us
    dot_general x4, matrix products, dot(): return jnp.dot(a, b, preferred_element_type=F32, **kw)  14.6 us
    pallas_call x1, Pallas kernels, scan_within(): pl.pallas_call(within_body, grid=(steps,), in_specs=[whole((rows, width))...  13 us
    ppermute x2, waiting for transfers between devices, far_shards(): lax.ppermute(kv, axis, [(i - k, i) for i in range(k, count)])  10.6 us
    pallas_call x1, Pallas kernels, scan_finish(): pl.pallas_call(finish_body, grid=(steps,), in_specs=[pl.BlockSpec((rows,...  9.33 us
    ppermute x2, waiting for transfers between devices, gather_main(): lax.ppermute(block, axis, [(i, (i + k) % count) for i in range(count)])  8.18 us
    ppermute x11, starting transfers between devices, sub_move(): return lax.ppermute(value, axis, route)  8.16 us
    pallas_call x1, Pallas kernels, scan_states(): pl.pallas_call(states_body, grid=(steps,), in_specs=[whole((rows, width))...  7.95 us
  transfers between devices with their start and end apart: 27, of which 11 were waited for; matrix products, arithmetic and copies ran while one was open for 13% of the time, Pallas kernels for 25%

profile of v1, /device:TPU:5, one launch (start us, length us, event | category | flops | bytes accessed | tf_op | source)
XLA Modules:
  0.0 170.7 jit_solution(2432878749154399680)
XLA Ops:
  0.0 7.9 %scan_states.1 = (bf16[512,1024]{1,0:T(8,128)(2,1)}, bf16[512,2048]{1,0:T(8,128)(2,1)}, bf16[512,256]{1,0:T(8,128)(2,1)}, f32[512,128]{1,0:T(8,128)}, f32[512,12...) custom-call(bf16[512,1024]{1,0:T(8,128)(2,1)} %bytes_ref.3, f32[1,1024]{1,0:T(1,128)} %bitcast.46, ...), custom_call_target="tpu_custom_call" | custom-call | flops 5400000000 | bytes 27000000 | tf_op jit(solution)/shard_map/scan_states/pallas_call | solution.py:142
  8.0 6.4 %all-to-all-start = ((bf16[32,80,128]{2,1,0:T(8,128)(2,1)}), bf16[32,80,128]{2,1,0:T(8,128)(2,1)S(1)}, u32[]{:S(2)}, u32[]{:S(2)}) async-start(bf16[32,80,128]{2,1,0:T(8,128)(2,1)} %get-tuple-element.61), calls=%async_computation | async-start | bytes 1310720 | tf_op jit(solution)/shard_map/all_to_all | solution.py:708
  14.5 4.2 %copy.18 = bf16[256,8,2,384]{3,1,2,0:T(8,128)(2,1)} copy(bf16[256,8,2,384]{3,2,1,0:T(2,128)(2,1)} %bitcast.38) | data formatting | bytes 6291456
  20.4 13.0 %scan_within.1 = (bf16[512,2048]{1,0:T(8,128)(2,1)}, bf16[512,2048]{1,0:T(8,128)(2,1)}) custom-call(bf16[512,1024]{1,0:T(8,128)(2,1)} %get-tuple-element.62.normed_ref, bf16[1024,4096]{1,0:T(8,128)(2,1)} %wg_ref.1, bf16[512,2048]{1,0:T(8,128)(2,1)} %get-tuple-element.63.x_ref, bf16[512,256]{1,0:T(8,128)(2,1)} %get-tuple-element.64.bc_ref.c_ref, ...), custom_call_target="tpu_custom_call" | custom-call | flops 8400000000 | bytes 42000000 | tf_op jit(solution)/shard_map/scan_within/pallas_call | solution.py:269
  36.3 5.8 %all-to-all-start.1 = ((bf16[32,64,128]{2,1,0:T(8,128)(2,1)}), bf16[32,64,128]{2,1,0:T(8,128)(2,1)S(1)}, u32[]{:S(2)}, u32[]{:S(2)}) async-start(bf16[32,64,128]{2,1,0:T(8,128)(2,1)} %state_prefix.1), calls=%async_computation.1 | async-start | bytes 1048576 | tf_op jit(solution)/shard_map/all_to_all | solution.py:717
  43.3 7.7 %fusion.4.weight_ref = bf16[1024,768]{1,0:T(8,128)(2,1)} fusion(bf16[2048,768]{1,0:T(8,128)(2,1)} %bitcast.39, bf16[1024,2048]{1,0:T(8,128)(2,1)} %down_ref.1, f32[2048]{0:T(1024)S(1)} %copy-done.20), kind=kOutput, calls=%fused_computation.7 | convolution fusion | flops 3228303360 | bytes 8921088 | tf_op jit(solution)/shard_map/dot_general | solution.py:33
  51.1 6.4 %all-to-all-done.1 = bf16[32,64,128]{2,1,0:T(8,128)(2,1)S(1)} async-done(((bf16[32,64,128]{2,1,0:T(8,128)(2,1)}), bf16[32,64,128]{2,1,0:T(8,128)(2,1)S(1)}, u32[]{:S(2)}, u32[]{:S(2)}) %all-to-all-start.1) | async-done | bytes 524320 | tf_op jit(solution)/shard_map/all_to_all | solution.py:717
  57.6 3.1 %collective-permute-start.1 = (bf16[256,256]{1,0:T(8,128)(2,1)S(1)}, bf16[256,256]{1,0:T(8,128)(2,1)S(1)}, u32[]{:S(2)}, u32[]{:S(2)}) collective-permute-start(bf16[256,256]{1,0:T(8,128)(2,1)S(1)} %convolution_convert_fusion), channel_id=1, source_target_pairs={{0,6},{1,7},{2,0},{3,1},{4,2},{5,3},{6,4},{7,5},{8,14},{9,15},{10,... | collective-permute-start | bytes 393224 | tf_op jit(solution)/shard_map/ppermute | solution.py:386
  60.7 9.3 %scan_finish.1 = (bf16[512,1024]{1,0:T(8,128)(2,1)}, bf16[96,2048]{1,0:T(8,128)(2,1)}, bf16[96,1024]{1,0:T(8,128)(2,1)}) custom-call(bf16[512,2048]{1,0:T(8,128)(2,1)} %get-tuple-element.75.yg_ref, bf16[512,2048]{1,0:T(8,128)(2,1)} %get-tuple-element.76.grown_ref, bf16[512,256]{1,0:T(8,128)(2,1)} %get-tuple-element.64.bc_ref.c_ref, ...), custom_call_target="tpu_custom_call" | custom-call | flops 6000000000 | bytes 30000000 | tf_op jit(solution)/shard_map/scan_finish/pallas_call | solution.py:340
  70.7 3.3 %collective-permute-start.4 = (bf16[96,1024]{1,0:T(8,128)(2,1)}, bf16[96,1024]{1,0:T(8,128)(2,1)S(1)}, u32[]{:S(2)}, u32[]{:S(2)}) collective-permute-start(bf16[96,1024]{1,0:T(8,128)(2,1)} %get-tuple-element.86.refs_0_), channel_id=1, source_target_pairs={{0,6},{1,7},{2,0},{3,1},{4,2},{5,3},{6,4},{7,5},{8,14},{9,15},{10,... | collective-permute-start | bytes 589832 | tf_op jit(solution)/shard_map/ppermute | solution.py:386
  78.1 3.3 %collective-permute-done.4.refs_2_ = bf16[96,1024]{1,0:T(8,128)(2,1)S(1)} collective-permute-done((bf16[96,1024]{1,0:T(8,128)(2,1)}, bf16[96,1024]{1,0:T(8,128)(2,1)S(1)}, u32[]{:S(2)}, u32[]{:S(2)}) %collective-permute-start.4) | collective-permute-done | bytes 196640 | tf_op jit(solution)/shard_map/ppermute | solution.py:386
  81.9 10.2 %collective-permute-done.5.refs_3_ = bf16[96,1024]{1,0:T(8,128)(2,1)S(1)} collective-permute-done((bf16[96,1024]{1,0:T(8,128)(2,1)}, bf16[96,1024]{1,0:T(8,128)(2,1)S(1)}, u32[]{:S(2)}, u32[]{:S(2)}) %collective-permute-start.5) | collective-permute-done | bytes 196640 | tf_op jit(solution)/shard_map/ppermute | solution.py:386
  92.8 3.5 %project_qkv.2 = (bf16[384,256]{1,0:T(8,128)(2,1)}, bf16[384,512]{1,0:T(8,128)(2,1)}) custom-call(bf16[1024,768]{1,0:T(8,128)(2,1)} %fusion.4.weight_ref, bf16[96,1024]{1,0:T(8,128)(2,1)} %get-tuple-element.86.refs_0_, bf16[96,1024]{1,0:T(8,128)(2,1)} %copy-done.16, bf16[96,1024]{1,0:T(8,128)(2,1)} %copy-done.17, bf16[96,1024]{1,0:T(8,128)(2,1)} %copy-done.18), custom_call_target="tpu_custom_call" | custom-call | flops 2400000000 | bytes 12000000 | tf_op jit(solution)/shard_map/project_qkv/pallas_call | solution.py:456
  98.2 3.5 %project_qkv.3 = (bf16[384,256]{1,0:T(8,128)(2,1)}, bf16[384,512]{1,0:T(8,128)(2,1)}) custom-call(bf16[1024,768]{1,0:T(8,128)(2,1)} %fusion.4.weight_ref, bf16[96,1024]{1,0:T(8,128)(2,1)} %copy-done.15, bf16[96,1024]{1,0:T(8,128)(2,1)} %copy-done.19, bf16[96,1024]{1,0:T(8,128)(2,1)} %collective-permute-done.8.refs_2_, ...), custom_call_target="tpu_custom_call" | custom-call | flops 2400000000 | bytes 12000000 | tf_op jit(solution)/shard_map/project_qkv/pallas_call | solution.py:456
  106.7 6.8 %near_attention.1 = (bf16[768,256]{1,0:T(8,128)(2,1)}, f32[4,768,128]{2,1,0:T(8,128)}, f32[768,256]{1,0:T(8,128)}) custom-call(s32[13]{0:T(128)} %stack.55.index_ref, f32[4,1,768]{2,1,0:T(1,128)} %compare_select_fusion.bias_ref, bf16[384,256]{1,0:T(8,128)(2,1)} %get-tuple-element.94.refs_0_, bf16[384,256]{1,0:T(8,128)(2,1)} %get-tuple-element.95.refs_1_, ...), custom_call_target="tpu_custom_call" | custom-call | flops 5400000000 | bytes 27000000 | tf_op jit(solution)/shard_map/near_attention/pallas_call | solution.py:589
  113.5 2.2 %collective-permute-done.12.refs_0_ = bf16[384,512]{1,0:T(8,128)(2,1)S(1)} collective-permute-done((bf16[384,512]{1,0:T(8,128)(2,1)S(1)}, bf16[384,512]{1,0:T(8,128)(2,1)S(1)}, u32[]{:S(2)}, u32[]{:S(2)}) %collective-permute-start.12) | collective-permute-done | bytes 393248 | tf_op jit(solution)/shard_map/ppermute | solution.py:664
  115.7 8.3 %collective-permute-done.13.refs_1_ = bf16[384,512]{1,0:T(8,128)(2,1)S(1)} collective-permute-done((bf16[384,512]{1,0:T(8,128)(2,1)}, bf16[384,512]{1,0:T(8,128)(2,1)S(1)}, u32[]{:S(2)}, u32[]{:S(2)}) %collective-permute-start.13) | collective-permute-done | bytes 393248 | tf_op jit(solution)/shard_map/ppermute | solution.py:664
  127.8 7.4 %far_attention.1 = bf16[768,256]{1,0:T(8,128)(2,1)} custom-call(s32[13]{0:T(128)} %stack.55.index_ref, bf16[768,256]{1,0:T(8,128)(2,1)} %get-tuple-element.103.q_ref, f32[4,768,128]{2,1,0:T(8,128)} %get-tuple-element.106.stats_in, f32[768,256]{1,0:T(8,128)} %get-tuple-element.107.acc_in, f32[4,1,768]{2,1,0:T(1,128)} %compare_select_fusion.bias_ref, ...), custom_call_target="tpu_custom_call" | custom-call | flops 5400000000 | bytes 27000000 | tf_op jit(solution)/shard_map/far_attention/pallas_call | solution.py:649
  135.3 4.5 %all-to-all-start.2 = ((bf16[8,96,256]{2,1,0:T(8,128)(2,1)}), bf16[8,96,256]{2,1,0:T(8,128)(2,1)S(1)}, u32[]{:S(2)}, u32[]{:S(2)}) async-start(bf16[8,96,256]{2,1,0:T(8,128)(2,1)} %bitcast.41), calls=%async_computation.2 | async-start | bytes 786432 | tf_op jit(solution)/shard_map/all_to_all | solution.py:775
  141.5 8.2 %collective-permute-done.20.refs_5_ = bf16[1024,256]{1,0:T(8,128)(2,1)} collective-permute-done((bf16[1024,256]{1,0:T(8,128)(2,1)}, bf16[1024,256]{1,0:T(8,128)(2,1)}, u32[]{:S(2)}, u32[]{:S(2)}) %collective-permute-start.20) | collective-permute-done | bytes 524320 | tf_op jit(solution)/shard_map/ppermute | solution.py:425
  150.9 3.8 %fusion.13.main_up_ref = f32[96,1024]{1,0:T(8,128)} fusion(bf16[96,2048]{1,0:T(8,128)(2,1)S(1)} %copy-done.4, bf16[2048,1024]{1,0:T(8,128)(2,1)} %param.33), kind=kOutput, calls=%fused_computation.33 | convolution fusion | flops 402653184 | bytes 4980736 | tf_op jit(solution)/shard_map/dot_general | solution.py:33
  156.2 4.7 %project_up.1 = (bf16[96,1024]{1,0:T(8,128)(2,1)}, bf16[16,1024]{1,0:T(8,128)(2,1)}) custom-call(s32[13]{0:T(128)} %stack.55.index_ref, s32[1]{0:T(128)} %bitcast.25.edge_ref, f32[96,1024]{1,0:T(8,128)} %fusion.13.main_up_ref, bf16[8,96,256]{2,1,0:T(8,128)(2,1)} %copy-done.5, bf16[1024,256]{1,0:T(8,128)(2,1)} %copy-done.6, ...), custom_call_target="tpu_custom_call" | custom-call | flops 3000000000 | bytes 15000000 | tf_op jit(solution)/shard_map/project_up/pallas_call | solution.py:502
  160.8 3.1 %collective-permute-start.23 = (bf16[16,1024]{1,0:T(8,128)(2,1)}, bf16[16,1024]{1,0:T(8,128)(2,1)S(1)}, u32[]{:S(2)}, u32[]{:S(2)}) collective-permute-start(bf16[16,1024]{1,0:T(8,128)(2,1)} %get-tuple-element.112), channel_id=1, source_target_pairs={{0,1},{1,2},{2,3},{3,4},{4,5},{5,6},{6,7},{7,8},{8,9},{9,10},{10,1... | collective-permute-start | bytes 98312 | tf_op jit(solution)/shard_map/ppermute | solution.py:777
  165.3 3.9 %collective-permute-done.23 = bf16[16,1024]{1,0:T(8,128)(2,1)S(1)} collective-permute-done((bf16[16,1024]{1,0:T(8,128)(2,1)}, bf16[16,1024]{1,0:T(8,128)(2,1)S(1)}, u32[]{:S(2)}, u32[]{:S(2)}) %collective-permute-start.23) | collective-permute-done | bytes 32800 | tf_op jit(solution)/shard_map/ppermute | solution.py:777
  (106 shorter events, 29.8 us)
Async XLA Ops:
  8.0 25.4 %all-to-all-start = ((bf16[32,80,128]{2,1,0:T(8,128)(2,1)}), bf16[32,80,128]{2,1,0:T(8,128)(2,1)S(1)}, u32[]{:S(2)}, u32[]{:S(2)}) async-start(bf16[32,80,128]{2,1,0:T(8,128)(2,1)} %get-tuple-element.61), calls=%async_computation | async-start | bytes 1310720 | tf_op jit(solution)/shard_map/all_to_all | solution.py:708
  36.3 21.1 %all-to-all-start.1 = ((bf16[32,64,128]{2,1,0:T(8,128)(2,1)}), bf16[32,64,128]{2,1,0:T(8,128)(2,1)S(1)}, u32[]{:S(2)}, u32[]{:S(2)}) async-start(bf16[32,64,128]{2,1,0:T(8,128)(2,1)} %state_prefix.1), calls=%async_computation.1 | async-start | bytes 1048576 | tf_op jit(solution)/shard_map/all_to_all | solution.py:717
  57.4 12.6 %collective-permute-start = (bf16[256,256]{1,0:T(8,128)(2,1)S(1)}, bf16[256,256]{1,0:T(8,128)(2,1)S(1)}, u32[]{:S(2)}, u32[]{:S(2)}) collective-permute-start(bf16[256,256]{1,0:T(8,128)(2,1)S(1)} %convolution_convert_fusion), channel_id=1, source_target_pairs={{0,2},{1,3},{2,4},{3,5},{4,6},{5,7},{6,0},{7,1},{8,10},{9,11},{10,... | collective-permute-start | bytes 393224 | tf_op jit(solution)/shard_map/ppermute | solution.py:386
  57.6 12.4 %collective-permute-start.1 = (bf16[256,256]{1,0:T(8,128)(2,1)S(1)}, bf16[256,256]{1,0:T(8,128)(2,1)S(1)}, u32[]{:S(2)}, u32[]{:S(2)}) collective-permute-start(bf16[256,256]{1,0:T(8,128)(2,1)S(1)} %convolution_convert_fusion), channel_id=1, source_target_pairs={{0,6},{1,7},{2,0},{3,1},{4,2},{5,3},{6,4},{7,5},{8,14},{9,15},{10,... | collective-permute-start | bytes 393224 | tf_op jit(solution)/shard_map/ppermute | solution.py:386
  60.7 10.0 %collective-permute-start.2 = (bf16[256,256]{1,0:T(8,128)(2,1)S(1)}, bf16[256,256]{1,0:T(8,128)(2,1)S(1)}, u32[]{:S(2)}, u32[]{:S(2)}) collective-permute-start(bf16[256,256]{1,0:T(8,128)(2,1)S(1)} %convolution_convert_fusion), channel_id=1, source_target_pairs={{0,4},{1,5},{2,6},{3,7},{4,0},{5,1},{6,2},{7,3},{8,12},{9,13},{10,... | collective-permute-start | bytes 393224 | tf_op jit(solution)/shard_map/ppermute | solution.py:386
  70.7 7.2 %collective-permute-start.3 = (bf16[96,1024]{1,0:T(8,128)(2,1)}, bf16[96,1024]{1,0:T(8,128)(2,1)S(1)}, u32[]{:S(2)}, u32[]{:S(2)}) collective-permute-start(bf16[96,1024]{1,0:T(8,128)(2,1)} %get-tuple-element.86.refs_0_), channel_id=1, source_target_pairs={{0,2},{1,3},{2,4},{3,5},{4,6},{5,7},{6,0},{7,1},{8,10},{9,11},{10,... | collective-permute-start | bytes 589832 | tf_op jit(solution)/shard_map/ppermute | solution.py:386
  70.7 10.8 %collective-permute-start.4 = (bf16[96,1024]{1,0:T(8,128)(2,1)}, bf16[96,1024]{1,0:T(8,128)(2,1)S(1)}, u32[]{:S(2)}, u32[]{:S(2)}) collective-permute-start(bf16[96,1024]{1,0:T(8,128)(2,1)} %get-tuple-element.86.refs_0_), channel_id=1, source_target_pairs={{0,6},{1,7},{2,0},{3,1},{4,2},{5,3},{6,4},{7,5},{8,14},{9,15},{10,... | collective-permute-start | bytes 589832 | tf_op jit(solution)/shard_map/ppermute | solution.py:386
  73.9 18.2 %collective-permute-start.5 = (bf16[96,1024]{1,0:T(8,128)(2,1)}, bf16[96,1024]{1,0:T(8,128)(2,1)S(1)}, u32[]{:S(2)}, u32[]{:S(2)}) collective-permute-start(bf16[96,1024]{1,0:T(8,128)(2,1)} %get-tuple-element.86.refs_0_), channel_id=1, source_target_pairs={{0,4},{1,5},{2,6},{3,7},{4,0},{5,1},{6,2},{7,3},{8,12},{9,13},{10,... | collective-permute-start | bytes 589832 | tf_op jit(solution)/shard_map/ppermute | solution.py:386
  73.9 22.8 %collective-permute-start.6 = (bf16[96,1024]{1,0:T(8,128)(2,1)}, bf16[96,1024]{1,0:T(8,128)(2,1)S(1)}, u32[]{:S(2)}, u32[]{:S(2)}) collective-permute-start(bf16[96,1024]{1,0:T(8,128)(2,1)} %get-tuple-element.86.refs_0_), channel_id=1, source_target_pairs={{0,1},{1,0},{2,3},{3,2},{4,5},{5,4},{6,7},{7,6},{8,9},{9,8},{10,11... | collective-permute-start | bytes 589832 | tf_op jit(solution)/shard_map/ppermute | solution.py:386
  77.9 18.9 %collective-permute-start.7 = (bf16[96,1024]{1,0:T(8,128)(2,1)S(1)}, bf16[96,1024]{1,0:T(8,128)(2,1)S(1)}, u32[]{:S(2)}, u32[]{:S(2)}) collective-permute-start(bf16[96,1024]{1,0:T(8,128)(2,1)S(1)} %collective-permute-done.3.refs_1_), channel_id=1, source_target_pairs={{0,1},{1,0},{2,3},{3,2},{4,5},{5,4},{6,7},{7,6},{8,9},{9,8},{10,11... | collective-permute-start | bytes 589832 | tf_op jit(solution)/shard_map/ppermute | solution.py:386
  81.4 15.4 %collective-permute-start.8 = (bf16[96,1024]{1,0:T(8,128)(2,1)S(1)}, bf16[96,1024]{1,0:T(8,128)(2,1)}, u32[]{:S(2)}, u32[]{:S(2)}) collective-permute-start(bf16[96,1024]{1,0:T(8,128)(2,1)S(1)} %collective-permute-done.4.refs_2_), channel_id=1, source_target_pairs={{0,1},{1,0},{2,3},{3,2},{4,5},{5,4},{6,7},{7,6},{8,9},{9,8},{10,11... | collective-permute-start | bytes 589832 | tf_op jit(solution)/shard_map/ppermute | solution.py:386
  92.1 6.1 %collective-permute-start.9 = (bf16[96,1024]{1,0:T(8,128)(2,1)S(1)}, bf16[96,1024]{1,0:T(8,128)(2,1)}, u32[]{:S(2)}, u32[]{:S(2)}) collective-permute-start(bf16[96,1024]{1,0:T(8,128)(2,1)S(1)} %collective-permute-done.5.refs_3_), channel_id=1, source_target_pairs={{0,1},{1,0},{2,3},{3,2},{4,5},{5,4},{6,7},{7,6},{8,9},{9,8},{10,11... | collective-permute-start | bytes 589832 | tf_op jit(solution)/shard_map/ppermute | solution.py:386
  96.3 9.6 %collective-permute-start.10 = (bf16[384,512]{1,0:T(8,128)(2,1)}, bf16[384,512]{1,0:T(8,128)(2,1)S(1)}, u32[]{:S(2)}, u32[]{:S(2)}) collective-permute-start(bf16[384,512]{1,0:T(8,128)(2,1)} %get-tuple-element.96.refs_2_), channel_id=1, source_target_pairs={{0,8},{8,0},{16,24},{24,16},{1,9},{9,1},{17,25},{25,17},{2,10},{10... | collective-permute-start | bytes 1179656 | tf_op jit(solution)/shard_map/ppermute | solution.py:419
  103.0 21.0 %collective-permute-start.14 = (bf16[1024,256]{1,0:T(8,128)(2,1)S(1)}, bf16[1024,256]{1,0:T(8,128)(2,1)}, u32[]{:S(2)}, u32[]{:S(2)}) collective-permute-start(bf16[1024,256]{1,0:T(8,128)(2,1)S(1)} %constant_dynamic-update-slice_fusion.refs_0_), channel_id=1, source_target_pairs={{0,1},{1,0},{2,3},{3,2},{4,5},{5,4},{6,7},{7,6},{8,9},{9,8},{10,11... | collective-permute-start | bytes 1572872 | tf_op jit(solution)/shard_map/ppermute | solution.py:386
  103.3 12.4 %collective-permute-start.12 = (bf16[384,512]{1,0:T(8,128)(2,1)S(1)}, bf16[384,512]{1,0:T(8,128)(2,1)S(1)}, u32[]{:S(2)}, u32[]{:S(2)}) collective-permute-start(bf16[384,512]{1,0:T(8,128)(2,1)S(1)} %copy-done.9), channel_id=1, source_target_pairs={{0,16},{8,24},{1,17},{9,25},{2,18},{10,26},{3,19},{11,27},{4,20},{... | collective-permute-start | bytes 1179656 | tf_op jit(solution)/shard_map/ppermute | solution.py:664
  104.6 19.4 %collective-permute-start.13 = (bf16[384,512]{1,0:T(8,128)(2,1)}, bf16[384,512]{1,0:T(8,128)(2,1)S(1)}, u32[]{:S(2)}, u32[]{:S(2)}) collective-permute-start(bf16[384,512]{1,0:T(8,128)(2,1)} %get-tuple-element.102.refs_3_), channel_id=1, source_target_pairs={{0,16},{8,24},{1,17},{9,25},{2,18},{10,26},{3,19},{11,27},{4,20},{... | collective-permute-start | bytes 1179656 | tf_op jit(solution)/shard_map/ppermute | solution.py:664
  125.3 15.7 %collective-permute-start.17 = (bf16[1024,256]{1,0:T(8,128)(2,1)S(1)}, bf16[1024,256]{1,0:T(8,128)(2,1)}, u32[]{:S(2)}, u32[]{:S(2)}) collective-permute-start(bf16[1024,256]{1,0:T(8,128)(2,1)S(1)} %constant_dynamic-update-slice_fusion.refs_0_), channel_id=1, source_target_pairs={{0,16},{8,24},{16,0},{24,8},{1,17},{9,25},{17,1},{25,9},{2,18},{10... | collective-permute-start | bytes 1572872 | tf_op jit(solution)/shard_map/ppermute | solution.py:425
  125.3 24.4 %collective-permute-start.20 = (bf16[1024,256]{1,0:T(8,128)(2,1)}, bf16[1024,256]{1,0:T(8,128)(2,1)}, u32[]{:S(2)}, u32[]{:S(2)}) collective-permute-start(bf16[1024,256]{1,0:T(8,128)(2,1)} %collective-permute-done.14.refs_4_), channel_id=1, source_target_pairs={{0,16},{8,24},{16,0},{24,8},{1,17},{9,25},{17,1},{25,9},{2,18},{10... | collective-permute-start | bytes 1572872 | tf_op jit(solution)/shard_map/ppermute | solution.py:425
  135.3 20.1 %all-to-all-start.2 = ((bf16[8,96,256]{2,1,0:T(8,128)(2,1)}), bf16[8,96,256]{2,1,0:T(8,128)(2,1)S(1)}, u32[]{:S(2)}, u32[]{:S(2)}) async-start(bf16[8,96,256]{2,1,0:T(8,128)(2,1)} %bitcast.41), calls=%async_computation.2 | async-start | bytes 786432 | tf_op jit(solution)/shard_map/all_to_all | solution.py:775
  139.9 15.5 %collective-permute-start.18 = (bf16[1024,256]{1,0:T(8,128)(2,1)S(1)}, bf16[1024,256]{1,0:T(8,128)(2,1)}, u32[]{:S(2)}, u32[]{:S(2)}) collective-permute-start(bf16[1024,256]{1,0:T(8,128)(2,1)S(1)} %constant_dynamic-update-slice_fusion.refs_0_), channel_id=1, source_target_pairs={{0,8},{8,0},{16,24},{24,16},{1,9},{9,1},{17,25},{25,17},{2,10},{10... | collective-permute-start | bytes 1572872 | tf_op jit(solution)/shard_map/ppermute | solution.py:419
  140.9 14.4 %collective-permute-start.19 = (bf16[1024,256]{1,0:T(8,128)(2,1)}, bf16[1024,256]{1,0:T(8,128)(2,1)}, u32[]{:S(2)}, u32[]{:S(2)}) collective-permute-start(bf16[1024,256]{1,0:T(8,128)(2,1)} %collective-permute-done.17.refs_1_), channel_id=1, source_target_pairs={{0,8},{8,0},{16,24},{24,16},{1,9},{9,1},{17,25},{25,17},{2,10},{10... | collective-permute-start | bytes 1572872 | tf_op jit(solution)/shard_map/ppermute | solution.py:419
  141.0 14.3 %collective-permute-start.21 = (bf16[1024,256]{1,0:T(8,128)(2,1)}, bf16[1024,256]{1,0:T(8,128)(2,1)}, u32[]{:S(2)}, u32[]{:S(2)}) collective-permute-start(bf16[1024,256]{1,0:T(8,128)(2,1)} %collective-permute-done.14.refs_4_), channel_id=1, source_target_pairs={{0,8},{8,0},{16,24},{24,16},{1,9},{9,1},{17,25},{25,17},{2,10},{10... | collective-permute-start | bytes 1572872 | tf_op jit(solution)/shard_map/ppermute | solution.py:419
  149.6 5.8 %collective-permute-start.22 = (bf16[1024,256]{1,0:T(8,128)(2,1)}, bf16[1024,256]{1,0:T(8,128)(2,1)}, u32[]{:S(2)}, u32[]{:S(2)}) collective-permute-start(bf16[1024,256]{1,0:T(8,128)(2,1)} %collective-permute-done.20.refs_5_), channel_id=1, source_target_pairs={{0,8},{8,0},{16,24},{24,16},{1,9},{9,1},{17,25},{25,17},{2,10},{10... | collective-permute-start | bytes 1572872 | tf_op jit(solution)/shard_map/ppermute | solution.py:419
  160.8 8.4 %collective-permute-start.23 = (bf16[16,1024]{1,0:T(8,128)(2,1)}, bf16[16,1024]{1,0:T(8,128)(2,1)S(1)}, u32[]{:S(2)}, u32[]{:S(2)}) collective-permute-start(bf16[16,1024]{1,0:T(8,128)(2,1)} %get-tuple-element.112), channel_id=1, source_target_pairs={{0,1},{1,2},{2,3},{3,4},{4,5},{5,6},{6,7},{7,8},{8,9},{9,10},{10,1... | collective-permute-start | bytes 98312 | tf_op jit(solution)/shard_map/ppermute | solution.py:777
  (24 other events, 215.5 us)

commit v2 on v1

--- a/solution.py
+++ b/solution.py
@@ -20,7 +20,7 @@
 WITHIN_STEP = 512
 STATE_STEP = 1024
 FINISH_STEP = 1024
-EXTRA = 16
+EXTRA = 8
 
 epsilon = 1e-06
 highest = lax.Precision.HIGHEST
@@ -392,7 +392,9 @@
 
 def gather_columns(block, axis):
     major, _ = sub_grid(lax.axis_size(axis))
-    return [block] + [sub_move(block, axis, dz, 0) for dz in places(major)[1:]]
+    *near, last = places(major)
+    near = [block] + [sub_move(block, axis, dz, 0) for dz in near[1:]]
+    return near + [sub_move(block, axis, last, 0)]
 
 
 def forward(value, axis):
@@ -743,7 +745,11 @@
     out_ups = [gather_main(out_up, "main")]
     columns = gather_columns(sent_rows, "sub")
     sub_index = sub_sources("sub")
-    index = jnp.stack([main_id] + main_sources("main") + sub_index).astype(jnp.int32)
+    major = len(columns)
+    early = [p for p in range(subs) if p < major - 1 or (p >= major and p % major == 0)]
+    order = early + [p for p in range(subs) if p not in early]
+    index = [main_id] + main_sources("main") + sub_index + [sub_index[p] for p in order]
+    index = jnp.stack(index).astype(jnp.int32)
     slot = jnp.arange(subs * CAP, dtype=jnp.int32)
     valid = slot[None] % CAP < jnp.repeat(counts.reshape(mains, subs), CAP, axis=1)
     bias = jnp.where(valid, 0.0, -1e30).astype(F32)[:, None, :]
@@ -753,7 +759,8 @@
     columns[1], index, bias = lax.optimization_barrier((columns[1], index, bias))
     pieces = gather_rest(columns, "sub")
     main_up = dot(main_in, up_proj)
-    groups = [pieces[: len(columns)], pieces[len(columns) :]]
+    pieces = [pieces[p] for p in order]
+    groups = [pieces[: len(early)], pieces[len(early) :]]
     projected = []
     for group in groups:
         projected.append(project_qkv(down_qkv, group))
@@ -765,7 +772,8 @@
     for kv in keys:
         far.append(far_shards(kv, "main"))
     q, stats, acc = near_attention(index, bias, [q for q, _ in projected], keys, others)
-    stats, far, *out_up = lax.optimization_barrier((stats, far, *out_up))
+    out_up = lax.optimization_barrier((far, out_up))[1]
+    stats, far = lax.optimization_barrier((stats, far))
     out_ups += [gather_main(part, "main") for part in out_up]
     shards = []
     for k in range(mains // 2 - 1):

time: 172 us -> 172 us (level)
    unnamed x46 -> x50, local copies, waits for them, and re-layouts: 7.72 us -> 7.97 us
where the time goes in v2:
time: 172 us; the launch traced here: 171 us
  Pallas kernels  58.2 us (34%)
  waiting for transfers between devices  48.1 us (28%)
  starting transfers between devices  36.6 us (21%)
  matrix products  14.6 us (8%)
  local copies, waits for them, and re-layouts  9.2 us (5%)
  other arithmetic  3.79 us (2%)
    ppermute x11, waiting for transfers between devices, sub_move(): return lax.ppermute(value, axis, route)  16.7 us
    dot_general x4, matrix products, dot(): return jnp.dot(a, b, preferred_element_type=F32, **kw)  14.6 us
    pallas_call x1, Pallas kernels, scan_within(): pl.pallas_call(within_body, grid=(steps,), in_specs=[whole((rows, width))...  13 us
    ppermute x2, waiting for transfers between devices, far_shards(): lax.ppermute(kv, axis, [(i - k, i) for i in range(k, count)])  11.2 us
    pallas_call x1, Pallas kernels, scan_finish(): pl.pallas_call(finish_body, grid=(steps,), in_specs=[pl.BlockSpec((rows,...  9.35 us
    ppermute x2, waiting for transfers between devices, gather_main(): lax.ppermute(block, axis, [(i, (i + k) % count) for i in range(count)])  8.54 us
    ppermute x11, starting transfers between devices, sub_move(): return lax.ppermute(value, axis, route)  8.24 us
    unnamed x50, local copies, waits for them, and re-layouts  7.97 us
  transfers between devices with their start and end apart: 27, of which 11 were waited for; matrix products, arithmetic and copies ran while one was open for 13% of the time, Pallas kernels for 25%

profile of v2, /device:TPU:5, one launch (start us, length us, event | category | flops | bytes accessed | tf_op | source)
XLA Modules:
  0.0 171.0 jit_solution(18167360028040161254)
XLA Ops:
  0.0 7.9 %scan_states.1 = (bf16[512,1024]{1,0:T(8,128)(2,1)}, bf16[512,2048]{1,0:T(8,128)(2,1)}, bf16[512,256]{1,0:T(8,128)(2,1)}, f32[512,128]{1,0:T(8,128)}, f32[512,12...) custom-call(bf16[512,1024]{1,0:T(8,128)(2,1)} %bytes_ref.3, f32[1,1024]{1,0:T(1,128)} %bitcast.46, ...), custom_call_target="tpu_custom_call" | custom-call | flops 5400000000 | bytes 27000000 | tf_op jit(solution)/shard_map/scan_states/pallas_call | solution.py:142
  7.9 6.4 %all-to-all-start = ((bf16[32,72,128]{2,1,0:T(8,128)(2,1)}), bf16[32,72,128]{2,1,0:T(8,128)(2,1)S(1)}, u32[]{:S(2)}, u32[]{:S(2)}) async-start(bf16[32,72,128]{2,1,0:T(8,128)(2,1)} %get-tuple-element.61), calls=%async_computation | async-start | bytes 1179648 | tf_op jit(solution)/shard_map/all_to_all | solution.py:710
  14.5 4.2 %copy.18 = bf16[256,8,2,384]{3,1,2,0:T(8,128)(2,1)} copy(bf16[256,8,2,384]{3,2,1,0:T(2,128)(2,1)} %bitcast.38) | data formatting | bytes 6291456
  20.4 13.0 %scan_within.1 = (bf16[512,2048]{1,0:T(8,128)(2,1)}, bf16[512,2048]{1,0:T(8,128)(2,1)}) custom-call(bf16[512,1024]{1,0:T(8,128)(2,1)} %get-tuple-element.62.normed_ref, bf16[1024,4096]{1,0:T(8,128)(2,1)} %wg_ref.1, bf16[512,2048]{1,0:T(8,128)(2,1)} %get-tuple-element.63.x_ref, bf16[512,256]{1,0:T(8,128)(2,1)} %get-tuple-element.64.bc_ref.c_ref, ...), custom_call_target="tpu_custom_call" | custom-call | flops 8400000000 | bytes 42000000 | tf_op jit(solution)/shard_map/scan_within/pallas_call | solution.py:269
  36.2 5.8 %all-to-all-start.1 = ((bf16[32,64,128]{2,1,0:T(8,128)(2,1)}), bf16[32,64,128]{2,1,0:T(8,128)(2,1)S(1)}, u32[]{:S(2)}, u32[]{:S(2)}) async-start(bf16[32,64,128]{2,1,0:T(8,128)(2,1)} %state_prefix.1), calls=%async_computation.1 | async-start | bytes 1048576 | tf_op jit(solution)/shard_map/all_to_all | solution.py:719
  43.2 7.7 %fusion.4.weight_ref = bf16[1024,768]{1,0:T(8,128)(2,1)} fusion(bf16[2048,768]{1,0:T(8,128)(2,1)} %bitcast.39, bf16[1024,2048]{1,0:T(8,128)(2,1)} %down_ref.1, f32[2048]{0:T(1024)S(1)} %copy-done.22), kind=kOutput, calls=%fused_computation.7 | convolution fusion | flops 3228303360 | bytes 8921088 | tf_op jit(solution)/shard_map/dot_general | solution.py:33
  51.0 6.4 %all-to-all-done.1 = bf16[32,64,128]{2,1,0:T(8,128)(2,1)S(1)} async-done(((bf16[32,64,128]{2,1,0:T(8,128)(2,1)}), bf16[32,64,128]{2,1,0:T(8,128)(2,1)S(1)}, u32[]{:S(2)}, u32[]{:S(2)}) %all-to-all-start.1) | async-done | bytes 524320 | tf_op jit(solution)/shard_map/all_to_all | solution.py:719
  57.6 3.1 %collective-permute-start.1 = (bf16[256,256]{1,0:T(8,128)(2,1)S(1)}, bf16[256,256]{1,0:T(8,128)(2,1)S(1)}, u32[]{:S(2)}, u32[]{:S(2)}) collective-permute-start(bf16[256,256]{1,0:T(8,128)(2,1)S(1)} %convolution_convert_fusion), channel_id=1, source_target_pairs={{0,6},{1,7},{2,0},{3,1},{4,2},{5,3},{6,4},{7,5},{8,14},{9,15},{10,... | collective-permute-start | bytes 393224 | tf_op jit(solution)/shard_map/ppermute | solution.py:386
  60.6 9.3 %scan_finish.1 = (bf16[512,1024]{1,0:T(8,128)(2,1)}, bf16[96,2048]{1,0:T(8,128)(2,1)}, bf16[96,1024]{1,0:T(8,128)(2,1)}) custom-call(bf16[512,2048]{1,0:T(8,128)(2,1)} %get-tuple-element.75.yg_ref, bf16[512,2048]{1,0:T(8,128)(2,1)} %get-tuple-element.76.grown_ref, bf16[512,256]{1,0:T(8,128)(2,1)} %get-tuple-element.64.bc_ref.c_ref, ...), custom_call_target="tpu_custom_call" | custom-call | flops 6000000000 | bytes 30000000 | tf_op jit(solution)/shard_map/scan_finish/pallas_call | solution.py:340
  70.6 3.3 %collective-permute-start.4 = (bf16[96,1024]{1,0:T(8,128)(2,1)}, bf16[96,1024]{1,0:T(8,128)(2,1)S(1)}, u32[]{:S(2)}, u32[]{:S(2)}) collective-permute-start(bf16[96,1024]{1,0:T(8,128)(2,1)} %get-tuple-element.86.refs_0_), channel_id=1, source_target_pairs={{0,6},{1,7},{2,0},{3,1},{4,2},{5,3},{6,4},{7,5},{8,14},{9,15},{10,... | collective-permute-start | bytes 589832 | tf_op jit(solution)/shard_map/ppermute | solution.py:386
  78.1 3.4 %collective-permute-done.4.refs_2_ = bf16[96,1024]{1,0:T(8,128)(2,1)S(1)} collective-permute-done((bf16[96,1024]{1,0:T(8,128)(2,1)}, bf16[96,1024]{1,0:T(8,128)(2,1)S(1)}, u32[]{:S(2)}, u32[]{:S(2)}) %collective-permute-start.4) | collective-permute-done | bytes 196640 | tf_op jit(solution)/shard_map/ppermute | solution.py:386
  81.9 10.2 %collective-permute-done.6.refs_0_ = bf16[96,1024]{1,0:T(8,128)(2,1)S(1)} collective-permute-done((bf16[96,1024]{1,0:T(8,128)(2,1)}, bf16[96,1024]{1,0:T(8,128)(2,1)S(1)}, u32[]{:S(2)}, u32[]{:S(2)}) %collective-permute-start.6) | collective-permute-done | bytes 196640 | tf_op jit(solution)/shard_map/ppermute | solution.py:386
  93.1 3.5 %project_qkv.2 = (bf16[384,256]{1,0:T(8,128)(2,1)}, bf16[384,512]{1,0:T(8,128)(2,1)}) custom-call(bf16[1024,768]{1,0:T(8,128)(2,1)} %fusion.4.weight_ref, bf16[96,1024]{1,0:T(8,128)(2,1)} %get-tuple-element.86.refs_0_, bf16[96,1024]{1,0:T(8,128)(2,1)} %copy-done.16, bf16[96,1024]{1,0:T(8,128)(2,1)} %copy-done.17, bf16[96,1024]{1,0:T(8,128)(2,1)} %copy-done.18), custom_call_target="tpu_custom_call" | custom-call | flops 2400000000 | bytes 12000000 | tf_op jit(solution)/shard_map/project_qkv/pallas_call | solution.py:458
  98.8 3.5 %project_qkv.3 = (bf16[384,256]{1,0:T(8,128)(2,1)}, bf16[384,512]{1,0:T(8,128)(2,1)}) custom-call(bf16[1024,768]{1,0:T(8,128)(2,1)} %fusion.4.weight_ref, bf16[96,1024]{1,0:T(8,128)(2,1)} %copy-done.15, bf16[96,1024]{1,0:T(8,128)(2,1)} %copy-done.19, bf16[96,1024]{1,0:T(8,128)(2,1)} %copy-done.20, bf16[96,1024]{1,0:T(8,128)(2,1)} %copy-done.21), custom_call_target="tpu_custom_call" | custom-call | flops 2400000000 | bytes 12000000 | tf_op jit(solution)/shard_map/project_qkv/pallas_call | solution.py:458
  106.5 6.8 %near_attention.1 = (bf16[768,256]{1,0:T(8,128)(2,1)}, f32[4,768,128]{2,1,0:T(8,128)}, f32[768,256]{1,0:T(8,128)}) custom-call(s32[21]{0:T(128)} %stack.63.index_ref, f32[4,1,768]{2,1,0:T(1,128)} %compare_select_fusion.bias_ref, bf16[384,256]{1,0:T(8,128)(2,1)} %get-tuple-element.94.refs_0_, bf16[384,256]{1,0:T(8,128)(2,1)} %get-tuple-element.95.refs_1_, ...), custom_call_target="tpu_custom_call" | custom-call | flops 5400000000 | bytes 27000000 | tf_op jit(solution)/shard_map/near_attention/pallas_call | solution.py:591
  113.3 2.8 %collective-permute-done.12.refs_0_ = bf16[384,512]{1,0:T(8,128)(2,1)S(1)} collective-permute-done((bf16[384,512]{1,0:T(8,128)(2,1)S(1)}, bf16[384,512]{1,0:T(8,128)(2,1)S(1)}, u32[]{:S(2)}, u32[]{:S(2)}) %collective-permute-start.12) | collective-permute-done | bytes 393248 | tf_op jit(solution)/shard_map/ppermute | solution.py:666
  116.1 8.4 %collective-permute-done.13.refs_1_ = bf16[384,512]{1,0:T(8,128)(2,1)S(1)} collective-permute-done((bf16[384,512]{1,0:T(8,128)(2,1)}, bf16[384,512]{1,0:T(8,128)(2,1)S(1)}, u32[]{:S(2)}, u32[]{:S(2)}) %collective-permute-start.13) | collective-permute-done | bytes 393248 | tf_op jit(solution)/shard_map/ppermute | solution.py:666
  128.1 7.4 %far_attention.1 = bf16[768,256]{1,0:T(8,128)(2,1)} custom-call(s32[21]{0:T(128)} %stack.63.index_ref, bf16[768,256]{1,0:T(8,128)(2,1)} %get-tuple-element.103.q_ref, f32[4,768,128]{2,1,0:T(8,128)} %get-tuple-element.105.stats_in, f32[768,256]{1,0:T(8,128)} %get-tuple-element.106.acc_in, f32[4,1,768]{2,1,0:T(1,128)} %compare_select_fusion.bias_ref, ...), custom_call_target="tpu_custom_call" | custom-call | flops 5400000000 | bytes 27000000 | tf_op jit(solution)/shard_map/far_attention/pallas_call | solution.py:651
  135.5 4.0 %all-to-all-start.2 = ((bf16[8,96,256]{2,1,0:T(8,128)(2,1)}), bf16[8,96,256]{2,1,0:T(8,128)(2,1)S(1)}, u32[]{:S(2)}, u32[]{:S(2)}) async-start(bf16[8,96,256]{2,1,0:T(8,128)(2,1)} %bitcast.41), calls=%async_computation.2 | async-start | bytes 786432 | tf_op jit(solution)/shard_map/all_to_all | solution.py:783
  141.2 8.5 %collective-permute-done.20.refs_5_ = bf16[1024,256]{1,0:T(8,128)(2,1)} collective-permute-done((bf16[1024,256]{1,0:T(8,128)(2,1)S(1)}, bf16[1024,256]{1,0:T(8,128)(2,1)}, u32[]{:S(2)}, u32[]{:S(2)}) %collective-permute-start.20) | collective-permute-done | bytes 524320 | tf_op jit(solution)/shard_map/ppermute | solution.py:427
  151.1 3.8 %fusion.13.main_up_ref = f32[96,1024]{1,0:T(8,128)} fusion(bf16[96,2048]{1,0:T(8,128)(2,1)S(1)} %copy-done.4, bf16[2048,1024]{1,0:T(8,128)(2,1)} %param.33), kind=kOutput, calls=%fused_computation.33 | convolution fusion | flops 402653184 | bytes 4980736 | tf_op jit(solution)/shard_map/dot_general | solution.py:33
  156.4 4.7 %project_up.1 = (bf16[96,1024]{1,0:T(8,128)(2,1)}, bf16[16,1024]{1,0:T(8,128)(2,1)}) custom-call(s32[21]{0:T(128)} %stack.63.index_ref, s32[1]{0:T(128)} %bitcast.25.edge_ref, f32[96,1024]{1,0:T(8,128)} %fusion.13.main_up_ref, bf16[8,96,256]{2,1,0:T(8,128)(2,1)} %copy-done.5, bf16[1024,256]{1,0:T(8,128)(2,1)} %copy-done.6, ...), custom_call_target="tpu_custom_call" | custom-call | flops 3000000000 | bytes 15000000 | tf_op jit(solution)/shard_map/project_up/pallas_call | solution.py:504
  161.1 2.2 %collective-permute-start.23 = (bf16[16,1024]{1,0:T(8,128)(2,1)}, bf16[16,1024]{1,0:T(8,128)(2,1)S(1)}, u32[]{:S(2)}, u32[]{:S(2)}) collective-permute-start(bf16[16,1024]{1,0:T(8,128)(2,1)} %get-tuple-element.112), channel_id=1, source_target_pairs={{0,1},{1,2},{2,3},{3,4},{4,5},{5,6},{6,7},{7,8},{8,9},{9,10},{10,1... | collective-permute-start | bytes 98312 | tf_op jit(solution)/shard_map/ppermute | solution.py:785
  164.7 4.8 %collective-permute-done.23 = bf16[16,1024]{1,0:T(8,128)(2,1)S(1)} collective-permute-done((bf16[16,1024]{1,0:T(8,128)(2,1)}, bf16[16,1024]{1,0:T(8,128)(2,1)S(1)}, u32[]{:S(2)}, u32[]{:S(2)}) %collective-permute-start.23) | collective-permute-done | bytes 32800 | tf_op jit(solution)/shard_map/ppermute | solution.py:785
  (110 shorter events, 29.4 us)
Async XLA Ops:
  7.9 25.4 %all-to-all-start = ((bf16[32,72,128]{2,1,0:T(8,128)(2,1)}), bf16[32,72,128]{2,1,0:T(8,128)(2,1)S(1)}, u32[]{:S(2)}, u32[]{:S(2)}) async-start(bf16[32,72,128]{2,1,0:T(8,128)(2,1)} %get-tuple-element.61), calls=%async_computation | async-start | bytes 1179648 | tf_op jit(solution)/shard_map/all_to_all | solution.py:710
  36.2 21.1 %all-to-all-start.1 = ((bf16[32,64,128]{2,1,0:T(8,128)(2,1)}), bf16[32,64,128]{2,1,0:T(8,128)(2,1)S(1)}, u32[]{:S(2)}, u32[]{:S(2)}) async-start(bf16[32,64,128]{2,1,0:T(8,128)(2,1)} %state_prefix.1), calls=%async_computation.1 | async-start | bytes 1048576 | tf_op jit(solution)/shard_map/all_to_all | solution.py:719
  57.4 12.6 %collective-permute-start = (bf16[256,256]{1,0:T(8,128)(2,1)S(1)}, bf16[256,256]{1,0:T(8,128)(2,1)S(1)}, u32[]{:S(2)}, u32[]{:S(2)}) collective-permute-start(bf16[256,256]{1,0:T(8,128)(2,1)S(1)} %convolution_convert_fusion), channel_id=1, source_target_pairs={{0,2},{1,3},{2,4},{3,5},{4,6},{5,7},{6,0},{7,1},{8,10},{9,11},{10,... | collective-permute-start | bytes 393224 | tf_op jit(solution)/shard_map/ppermute | solution.py:386
  57.6 12.4 %collective-permute-start.1 = (bf16[256,256]{1,0:T(8,128)(2,1)S(1)}, bf16[256,256]{1,0:T(8,128)(2,1)S(1)}, u32[]{:S(2)}, u32[]{:S(2)}) collective-permute-start(bf16[256,256]{1,0:T(8,128)(2,1)S(1)} %convolution_convert_fusion), channel_id=1, source_target_pairs={{0,6},{1,7},{2,0},{3,1},{4,2},{5,3},{6,4},{7,5},{8,14},{9,15},{10,... | collective-permute-start | bytes 393224 | tf_op jit(solution)/shard_map/ppermute | solution.py:386
  60.6 10.0 %collective-permute-start.2 = (bf16[256,256]{1,0:T(8,128)(2,1)S(1)}, bf16[256,256]{1,0:T(8,128)(2,1)S(1)}, u32[]{:S(2)}, u32[]{:S(2)}) collective-permute-start(bf16[256,256]{1,0:T(8,128)(2,1)S(1)} %convolution_convert_fusion), channel_id=1, source_target_pairs={{0,4},{1,5},{2,6},{3,7},{4,0},{5,1},{6,2},{7,3},{8,12},{9,13},{10,... | collective-permute-start | bytes 393224 | tf_op jit(solution)/shard_map/ppermute | solution.py:386
  70.6 7.2 %collective-permute-start.3 = (bf16[96,1024]{1,0:T(8,128)(2,1)}, bf16[96,1024]{1,0:T(8,128)(2,1)S(1)}, u32[]{:S(2)}, u32[]{:S(2)}) collective-permute-start(bf16[96,1024]{1,0:T(8,128)(2,1)} %get-tuple-element.86.refs_0_), channel_id=1, source_target_pairs={{0,2},{1,3},{2,4},{3,5},{4,6},{5,7},{6,0},{7,1},{8,10},{9,11},{10,... | collective-permute-start | bytes 589832 | tf_op jit(solution)/shard_map/ppermute | solution.py:386
  70.6 10.8 %collective-permute-start.4 = (bf16[96,1024]{1,0:T(8,128)(2,1)}, bf16[96,1024]{1,0:T(8,128)(2,1)S(1)}, u32[]{:S(2)}, u32[]{:S(2)}) collective-permute-start(bf16[96,1024]{1,0:T(8,128)(2,1)} %get-tuple-element.86.refs_0_), channel_id=1, source_target_pairs={{0,6},{1,7},{2,0},{3,1},{4,2},{5,3},{6,4},{7,5},{8,14},{9,15},{10,... | collective-permute-start | bytes 589832 | tf_op jit(solution)/shard_map/ppermute | solution.py:386
  73.9 18.5 %collective-permute-start.5 = (bf16[96,1024]{1,0:T(8,128)(2,1)}, bf16[96,1024]{1,0:T(8,128)(2,1)S(1)}, u32[]{:S(2)}, u32[]{:S(2)}) collective-permute-start(bf16[96,1024]{1,0:T(8,128)(2,1)} %get-tuple-element.86.refs_0_), channel_id=1, source_target_pairs={{0,1},{1,0},{2,3},{3,2},{4,5},{5,4},{6,7},{7,6},{8,9},{9,8},{10,11... | collective-permute-start | bytes 589832 | tf_op jit(solution)/shard_map/ppermute | solution.py:386
  74.2 17.9 %collective-permute-start.6 = (bf16[96,1024]{1,0:T(8,128)(2,1)}, bf16[96,1024]{1,0:T(8,128)(2,1)S(1)}, u32[]{:S(2)}, u32[]{:S(2)}) collective-permute-start(bf16[96,1024]{1,0:T(8,128)(2,1)} %get-tuple-element.86.refs_0_), channel_id=1, source_target_pairs={{0,4},{1,5},{2,6},{3,7},{4,0},{5,1},{6,2},{7,3},{8,12},{9,13},{10,... | collective-permute-start | bytes 589832 | tf_op jit(solution)/shard_map/ppermute | solution.py:386
  77.8 19.5 %collective-permute-start.7 = (bf16[96,1024]{1,0:T(8,128)(2,1)S(1)}, bf16[96,1024]{1,0:T(8,128)(2,1)S(1)}, u32[]{:S(2)}, u32[]{:S(2)}) collective-permute-start(bf16[96,1024]{1,0:T(8,128)(2,1)S(1)} %collective-permute-done.3.refs_1_), channel_id=1, source_target_pairs={{0,1},{1,0},{2,3},{3,2},{4,5},{5,4},{6,7},{7,6},{8,9},{9,8},{10,11... | collective-permute-start | bytes 589832 | tf_op jit(solution)/shard_map/ppermute | solution.py:386
  81.4 15.9 %collective-permute-start.8 = (bf16[96,1024]{1,0:T(8,128)(2,1)S(1)}, bf16[96,1024]{1,0:T(8,128)(2,1)S(1)}, u32[]{:S(2)}, u32[]{:S(2)}) collective-permute-start(bf16[96,1024]{1,0:T(8,128)(2,1)S(1)} %collective-permute-done.4.refs_2_), channel_id=1, source_target_pairs={{0,1},{1,0},{2,3},{3,2},{4,5},{5,4},{6,7},{7,6},{8,9},{9,8},{10,11... | collective-permute-start | bytes 589832 | tf_op jit(solution)/shard_map/ppermute | solution.py:386
  92.1 6.0 %collective-permute-start.9 = (bf16[96,1024]{1,0:T(8,128)(2,1)S(1)}, bf16[96,1024]{1,0:T(8,128)(2,1)S(1)}, u32[]{:S(2)}, u32[]{:S(2)}) collective-permute-start(bf16[96,1024]{1,0:T(8,128)(2,1)S(1)} %collective-permute-done.6.refs_0_), channel_id=1, source_target_pairs={{0,1},{1,0},{2,3},{3,2},{4,5},{5,4},{6,7},{7,6},{8,9},{9,8},{10,11... | collective-permute-start | bytes 589832 | tf_op jit(solution)/shard_map/ppermute | solution.py:386
  96.5 10.0 %collective-permute-start.10 = (bf16[384,512]{1,0:T(8,128)(2,1)}, bf16[384,512]{1,0:T(8,128)(2,1)}, u32[]{:S(2)}, u32[]{:S(2)}) collective-permute-start(bf16[384,512]{1,0:T(8,128)(2,1)} %get-tuple-element.96.refs_2_), channel_id=1, source_target_pairs={{0,8},{8,0},{16,24},{24,16},{1,9},{9,1},{17,25},{25,17},{2,10},{10... | collective-permute-start | bytes 1179656 | tf_op jit(solution)/shard_map/ppermute | solution.py:421
  103.6 12.5 %collective-permute-start.12 = (bf16[384,512]{1,0:T(8,128)(2,1)S(1)}, bf16[384,512]{1,0:T(8,128)(2,1)S(1)}, u32[]{:S(2)}, u32[]{:S(2)}) collective-permute-start(bf16[384,512]{1,0:T(8,128)(2,1)S(1)} %copy-done.11), channel_id=1, source_target_pairs={{0,16},{8,24},{1,17},{9,25},{2,18},{10,26},{3,19},{11,27},{4,20},{... | collective-permute-start | bytes 1179656 | tf_op jit(solution)/shard_map/ppermute | solution.py:666
  104.8 19.7 %collective-permute-start.13 = (bf16[384,512]{1,0:T(8,128)(2,1)}, bf16[384,512]{1,0:T(8,128)(2,1)S(1)}, u32[]{:S(2)}, u32[]{:S(2)}) collective-permute-start(bf16[384,512]{1,0:T(8,128)(2,1)} %get-tuple-element.102.refs_3_), channel_id=1, source_target_pairs={{0,16},{8,24},{1,17},{9,25},{2,18},{10,26},{3,19},{11,27},{4,20},{... | collective-permute-start | bytes 1179656 | tf_op jit(solution)/shard_map/ppermute | solution.py:666
  106.1 19.3 %collective-permute-start.19 = (bf16[1024,256]{1,0:T(8,128)(2,1)S(1)}, bf16[1024,256]{1,0:T(8,128)(2,1)S(1)}, u32[]{:S(2)}, u32[]{:S(2)}) collective-permute-start(bf16[1024,256]{1,0:T(8,128)(2,1)S(1)} %constant_dynamic-update-slice_fusion.refs_0_), channel_id=1, source_target_pairs={{0,1},{1,0},{2,3},{3,2},{4,5},{5,4},{6,7},{7,6},{8,9},{9,8},{10,11... | collective-permute-start | bytes 1572872 | tf_op jit(solution)/shard_map/ppermute | solution.py:386
  125.4 15.3 %collective-permute-start.16 = (bf16[1024,256]{1,0:T(8,128)(2,1)S(1)}, bf16[1024,256]{1,0:T(8,128)(2,1)}, u32[]{:S(2)}, u32[]{:S(2)}) collective-permute-start(bf16[1024,256]{1,0:T(8,128)(2,1)S(1)} %constant_dynamic-update-slice_fusion.refs_0_), channel_id=1, source_target_pairs={{0,16},{8,24},{16,0},{24,8},{1,17},{9,25},{17,1},{25,9},{2,18},{10... | collective-permute-start | bytes 1572872 | tf_op jit(solution)/shard_map/ppermute | solution.py:427
  125.4 24.3 %collective-permute-start.20 = (bf16[1024,256]{1,0:T(8,128)(2,1)S(1)}, bf16[1024,256]{1,0:T(8,128)(2,1)}, u32[]{:S(2)}, u32[]{:S(2)}) collective-permute-start(bf16[1024,256]{1,0:T(8,128)(2,1)S(1)} %collective-permute-done.19.refs_4_), channel_id=1, source_target_pairs={{0,16},{8,24},{16,0},{24,8},{1,17},{9,25},{17,1},{25,9},{2,18},{10... | collective-permute-start | bytes 1572872 | tf_op jit(solution)/shard_map/ppermute | solution.py:427
  135.5 20.1 %all-to-all-start.2 = ((bf16[8,96,256]{2,1,0:T(8,128)(2,1)}), bf16[8,96,256]{2,1,0:T(8,128)(2,1)S(1)}, u32[]{:S(2)}, u32[]{:S(2)}) async-start(bf16[8,96,256]{2,1,0:T(8,128)(2,1)} %bitcast.41), calls=%async_computation.2 | async-start | bytes 786432 | tf_op jit(solution)/shard_map/all_to_all | solution.py:783
  139.6 16.0 %collective-permute-start.17 = (bf16[1024,256]{1,0:T(8,128)(2,1)S(1)}, bf16[1024,256]{1,0:T(8,128)(2,1)}, u32[]{:S(2)}, u32[]{:S(2)}) collective-permute-start(bf16[1024,256]{1,0:T(8,128)(2,1)S(1)} %constant_dynamic-update-slice_fusion.refs_0_), channel_id=1, source_target_pairs={{0,8},{8,0},{16,24},{24,16},{1,9},{9,1},{17,25},{25,17},{2,10},{10... | collective-permute-start | bytes 1572872 | tf_op jit(solution)/shard_map/ppermute | solution.py:421
  140.7 14.9 %collective-permute-start.18 = (bf16[1024,256]{1,0:T(8,128)(2,1)}, bf16[1024,256]{1,0:T(8,128)(2,1)}, u32[]{:S(2)}, u32[]{:S(2)}) collective-permute-start(bf16[1024,256]{1,0:T(8,128)(2,1)} %collective-permute-done.16.refs_1_), channel_id=1, source_target_pairs={{0,8},{8,0},{16,24},{24,16},{1,9},{9,1},{17,25},{25,17},{2,10},{10... | collective-permute-start | bytes 1572872 | tf_op jit(solution)/shard_map/ppermute | solution.py:421
  140.8 14.8 %collective-permute-start.21 = (bf16[1024,256]{1,0:T(8,128)(2,1)S(1)}, bf16[1024,256]{1,0:T(8,128)(2,1)}, u32[]{:S(2)}, u32[]{:S(2)}) collective-permute-start(bf16[1024,256]{1,0:T(8,128)(2,1)S(1)} %collective-permute-done.19.refs_4_), channel_id=1, source_target_pairs={{0,8},{8,0},{16,24},{24,16},{1,9},{9,1},{17,25},{25,17},{2,10},{10... | collective-permute-start | bytes 1572872 | tf_op jit(solution)/shard_map/ppermute | solution.py:421
  149.7 5.9 %collective-permute-start.22 = (bf16[1024,256]{1,0:T(8,128)(2,1)}, bf16[1024,256]{1,0:T(8,128)(2,1)}, u32[]{:S(2)}, u32[]{:S(2)}) collective-permute-start(bf16[1024,256]{1,0:T(8,128)(2,1)} %collective-permute-done.20.refs_5_), channel_id=1, source_target_pairs={{0,8},{8,0},{16,24},{24,16},{1,9},{9,1},{17,25},{25,17},{2,10},{10... | collective-permute-start | bytes 1572872 | tf_op jit(solution)/shard_map/ppermute | solution.py:421
  161.1 8.4 %collective-permute-start.23 = (bf16[16,1024]{1,0:T(8,128)(2,1)}, bf16[16,1024]{1,0:T(8,128)(2,1)S(1)}, u32[]{:S(2)}, u32[]{:S(2)}) collective-permute-start(bf16[16,1024]{1,0:T(8,128)(2,1)} %get-tuple-element.112), channel_id=1, source_target_pairs={{0,1},{1,2},{2,3},{3,4},{4,5},{5,6},{6,7},{7,8},{8,9},{9,10},{10,1... | collective-permute-start | bytes 98312 | tf_op jit(solution)/shard_map/ppermute | solution.py:785
  (26 other events, 231.4 us)
